TPU v7x, 128 devices: a whole 4x4x4 slice. The times are simulated.
128 devices in a mesh: gen: 4 (over z), learn: 32 (over x, y, core).
Axes of the slice: x: 4, y: 4, z: 4, core: 2. Of those that a mesh axis runs over, the one named last changes fastest.
Arguments:
- hidden: bfloat16 [32768, 5120], P(('gen', 'learn')), may hold values from -0.59765625 to 0.59765625
- cotangent: bfloat16 [32768, 1024], P(('gen', 'learn')), may hold values from -0.29882812 to 0.29882812
- importance: float32 [32768], P(('gen', 'learn')), may hold values from 0.25 to 4
- block_len: int32 [4096], P(('gen', 'learn')), may hold values from 1 to 8
- version: int32 [4096], P(('gen', 'learn')), may hold values from 0 to 3
- destination: int32 [4096, 1], P(('gen', 'learn')), may hold values from 0 to 31; in each aligned block of 32 rows (0 to 31, 32 to 63, ...) at most 2 rows name the same one
- w_key: bfloat16 [5120, 1024], replicated, may hold values from -0.078125 to 0.078125
- in_gain: float32 [5120], replicated, may hold values from 0.5 to 1.5
- key_gain: float32 [128], replicated, may hold values from 0.5 to 1.5
Outputs:
- grad_slots: bfloat16 [65536, 5120], P(('gen', 'learn'))
- w_grad: float32 [5120, 1024], P('gen')
- gain_grad: float32 [5120], replicated
- kgain_grad: float32 [128], replicated
Inputs may be any that keep to these rules, and one draw needn't show every extreme that they name: `destination`: the 32 blocks of one device name each learner at most 2 times.
All inputs are finite; a program needn't handle non-finite values.
Results may differ from a plain program's by a relative error of at most 0.0075.
Values may be sent and summed in bfloat16 or wider, within the bound.
A program may use at most 128 MiB of HBM per device.

v0:
```python
import jax
import jax.numpy as jnp
from jax import lax
from jax.sharding import PartitionSpec as P

TILE = 8
VERSIONS = 4
SLOTS = 64


epsilon = 1e-06
clip_ratio = 2.0
staleness = 0.5


def packed_total(arrays, axis):
    ends = [0]
    for a in arrays:
        ends.append(ends[-1] + a.size)
    so_far = lax.psum(jnp.concatenate([a.ravel() for a in arrays]), axis)
    return tuple((so_far[b:e].reshape(a.shape) for a, b, e in zip(arrays, ends, ends[1:])))


def token_weights(importance, block_len, version):
    tile_count = block_len.shape[0]
    inside = (lax.broadcasted_iota(jnp.int32, (tile_count, TILE), 1) < block_len[:, None]).astype(
        jnp.float32
    )
    stale_age = (VERSIONS - 1 - version).astype(jnp.float32)
    decay_factor = jnp.power(jnp.float32(staleness), stale_age)
    return jnp.minimum(importance, clip_ratio) * (decay_factor[:, None] * inside).reshape(-1)


def layer_pass(hidden, upstream_rows, w_key, in_gain, key_gain):
    row_count = hidden.shape[0]
    x_float = hidden.astype(jnp.float32)
    inv_rms = lax.rsqrt(jnp.mean(x_float * x_float, -1, keepdims=True) + epsilon)
    normed = x_float * inv_rms
    h_rows = (normed * in_gain).astype(jnp.bfloat16)
    key_rows = jnp.dot(h_rows, w_key, preferred_element_type=jnp.float32).reshape(
        row_count, -1, key_gain.shape[0]
    )
    key_scale = lax.rsqrt(jnp.mean(key_rows * key_rows, -1, keepdims=True) + epsilon)
    upstream = upstream_rows.astype(jnp.float32).reshape(key_rows.shape)
    kgain_part = jnp.sum(upstream * key_rows * key_scale, axis=(0, 1))
    scaled = upstream * key_gain
    grad_keys = key_scale * scaled - key_rows * key_scale**3 * jnp.mean(
        scaled * key_rows, -1, keepdims=True
    )
    grad_keys = grad_keys.reshape(row_count, -1).astype(jnp.bfloat16)
    grad_h = lax.dot_general(
        grad_keys, w_key, (((1,), (1,)), ((), ())), preferred_element_type=jnp.float32
    )
    gain_part = jnp.sum(grad_h * normed, 0)
    grad_normed = grad_h * in_gain
    grad_input = inv_rms * (
        grad_normed - normed * jnp.mean(grad_normed * normed, -1, keepdims=True)
    )
    return (grad_input.astype(jnp.bfloat16), h_rows, grad_keys, gain_part, kgain_part)


def body(hidden, cotangent, importance, block_len, version, destination, w_key, in_gain, key_gain):
    learners = lax.axis_size("learn")
    generators = lax.axis_size("gen")
    capacity = SLOTS // learners
    tile_count = block_len.shape[0]
    model_width = hidden.shape[1]
    weights = token_weights(importance, block_len, version)
    upstream_all = (cotangent.astype(jnp.float32) * weights[:, None]).astype(jnp.bfloat16)
    dest_column = destination[:, 0]
    onehot = (dest_column[:, None] == jnp.arange(learners, dtype=jnp.int32)[None, :]).astype(
        jnp.int32
    )
    slot_rank = jnp.sum((jnp.cumsum(onehot, 0) - onehot) * onehot, 1)
    target = dest_column * capacity + slot_rank
    placing = (target[None, :] == jnp.arange(SLOTS, dtype=jnp.int32)[:, None]).astype(jnp.bfloat16)
    grad_local, h_rows, grad_keys, gain_part, kgain_part = layer_pass(
        hidden, upstream_all, w_key, in_gain, key_gain
    )
    feature_count = grad_local.shape[1]
    spread = jnp.dot(
        placing,
        grad_local.reshape(tile_count, TILE * feature_count),
        preferred_element_type=jnp.float32,
    )
    grad_slots = lax.all_to_all(
        spread.astype(jnp.bfloat16).reshape(SLOTS * TILE, feature_count),
        "learn",
        split_axis=0,
        concat_axis=0,
        tiled=True,
    )
    row_count = h_rows.shape[0]
    group_width = model_width // generators
    sliced = h_rows.reshape(row_count, generators, group_width)
    arrived_rows = lax.all_to_all(sliced, "gen", split_axis=1, concat_axis=0, tiled=True).reshape(
        generators * row_count, group_width
    )
    gathered_keys = lax.all_gather(grad_keys, "gen", axis=0, tiled=True)
    partial_rows = lax.dot_general(
        arrived_rows, gathered_keys, (((0,), (0,)), ((), ())), preferred_element_type=jnp.float32
    )
    w_grad = lax.psum(partial_rows, "learn")
    gain_grad, kgain_grad = packed_total((gain_part, kgain_part), ("gen", "learn"))
    return (grad_slots, w_grad, gain_grad, kgain_grad)


def solution(mesh):
    return jax.shard_map(
        body,
        mesh=mesh,
        in_specs=(
            P(("gen", "learn"), None),
            P(("gen", "learn"), None),
            P(("gen", "learn")),
            P(("gen", "learn")),
            P(("gen", "learn")),
            P(("gen", "learn"), None),
            P(),
            P(),
            P(),
        ),
        out_specs=(P(("gen", "learn"), None), P("gen", None), P(), P()),
        check_vma=False,
    )
```

profile of v0, /device:TPU:1, one launch (start us, length us, event | category | flops | bytes accessed | tf_op | source)
XLA Modules:
  0.0 262.8 jit_solution(8460036367396275193)
XLA Ops:
  7.2 2.3 fusion.10
  9.6 2.5 fusion.4
  12.1 6.5 %fusion.19 = f32[256,1024]{1,0:T(8,128)S(1)} fusion(bf16[256,5120]{1,0:T(8,128)(2,1)S(1)} %fusion.4, bf16[5120,1024]{1,0:T(8,128)(2,1)} %param.15), kind=kOutput, calls=%fused_computation.47 | convolution fusion | flops 2684354560 | bytes 14155776 | tf_op jit(solution)/shard_map/dot_general | solution.py:40
  18.7 0.2 copy.26
  19.0 0.1 mul.159
  19.1 0.1 convert_bitcast_fusion
  19.3 0.2 copy.29
  19.6 0.7 multiply_reduce_fusion.1
  20.4 0.1 copy.20
  20.5 0.1 copy.21
  20.7 0.1 copy.23
  20.9 0.3 mul.155
  21.2 0.3 mul.168
  21.5 0.3 mul.174
  21.9 1.8 fusion.15
  23.8 3.6 %copy.36 = bf16[32,4,8,1280]{3,2,0,1:T(8,128)(2,1)} copy(bf16[32,4,8,1280]{3,2,1,0:T(8,128)(2,1)} %bitcast.43) | data formatting | bytes 5242880 | tf_op jit(solution)/shard_map/reshape | solution.py:95
  27.3 5.8 %all-to-all-start.1 = ((bf16[256,4,1280]{2,0,1:T(8,128)(2,1)}), bf16[256,4,1280]{2,0,1:T(8,128)(2,1)}, u32[]{:S(2)}, u32[]{:S(2)}) async-start(bf16[256,4,1280]{2,0,1:T(8,128)(2,1)} %bitcast.44), calls=%async_computation.1 | async-start | bytes 5242880 | tf_op jit(solution)/shard_map/all_to_all | solution.py:96
  33.2 6.5 %fusion.9 = (f32[5120]{0:T(1024)S(1)}, f32[256]{0:T(256)S(1)}, f32[256,5120]{1,0:T(8,128)S(1)}) fusion(bf16[256,5120]{1,0:T(8,128)(2,1)S(1)} %copy-done, f32[256]{0:T(256)S(1)} %add_rsqrt_fusion.1, f32[5120]{0:T(1024)S(1)} %copy-done.5, bf16[256,1024]{1,0:T(8,128)(2,1)S(1)} %copy-done.3, bf16[5120,1024]{1,0:T(8,128)(2,1)} %param.15), kind=kOutput, calls=%fused_computation.12 | convolution fusion | flops 2693524224 | bytes 18917376 | tf_op jit(solution)/shard_map/dot_general | solution.py:51
  39.7 3.0 %fusion.8 = bf16[256,5120]{1,0:T(8,128)(2,1)} fusion(bf16[256,5120]{1,0:T(8,128)(2,1)S(1)} %copy-done, f32[256,5120]{1,0:T(8,128)S(1)} %get-tuple-element.12, f32[256]{0:T(256)S(1)} %broadcast_multiply_fusion.1, f32[5120]{0:T(1024)S(1)} %copy-done.5, f32[256]{0:T(256)S(1)} %add_rsqrt_fusion.1), kind=kLoop, calls=%fused_computation.11 | loop fusion | flops 9175040 | bytes 10508288 | tf_op jit(solution)/shard_map/convert_element_type | solution.py:59
  42.7 3.2 %reshape.87 = bf16[32,40960]{1,0:T(8,128)(2,1)S(1)} reshape(bf16[256,5120]{1,0:T(8,128)(2,1)} %fusion.8) | data formatting | bytes 5242880 | tf_op jit(solution)/shard_map/reshape | solution.py:83
  46.0 0.2 select_reduce_fusion
  46.2 3.9 %convolution_convert_fusion = bf16[64,40960]{1,0:T(8,128)(2,1)} fusion(bf16[32,40960]{1,0:T(8,128)(2,1)S(1)} %reshape.87, s32[32]{0:T(128)S(1)} %multiply_add_fusion), kind=kOutput, calls=%fused_computation | convolution fusion | flops 170395648 | bytes 7864448 | tf_op jit(solution)/shard_map/dot_general | solution.py:81
  50.1 8.1 %all_to_all.19 = bf16[32,16,5120]{2,1,0:T(8,128)(2,1)} reshape(bf16[64,40960]{1,0:T(8,128)(2,1)} %convolution_convert_fusion) | data formatting | bytes 10485760 | tf_op jit(solution)/shard_map/all_to_all | solution.py:86
  58.2 23.3 %all-to-all-done.1 = bf16[256,4,1280]{2,0,1:T(8,128)(2,1)} async-done(((bf16[256,4,1280]{2,0,1:T(8,128)(2,1)}), bf16[256,4,1280]{2,0,1:T(8,128)(2,1)}, u32[]{:S(2)}, u32[]{:S(2)}) %all-to-all-start.1) | async-done | bytes 2621472 | tf_op jit(solution)/shard_map/all_to_all | solution.py:96
  81.5 8.8 %all-to-all-start = ((bf16[32,16,5120]{2,1,0:T(8,128)(2,1)}), bf16[32,16,5120]{2,1,0:T(8,128)(2,1)}, u32[]{:S(2)}, u32[]{:S(2)}) async-start(bf16[32,16,5120]{2,1,0:T(8,128)(2,1)} %all_to_all.19), calls=%async_computation | async-start | bytes 10485760 | tf_op jit(solution)/shard_map/all_to_all | solution.py:86
  90.4 7.7 %fusion.20 = f32[1280,1024]{1,0:T(8,128)} fusion(bf16[1024,1280]{1,0:T(8,128)(2,1)} %bitcast.5, bf16[1024,1024]{1,0:T(8,128)(2,1)} %all-gather.2.cloned.1.call-done), kind=kOutput, calls=%fused_computation.48 | convolution fusion | flops 2684354560 | bytes 9961472 | tf_op jit(solution)/shard_map/dot_general | solution.py:100
  98.1 120.7 %psum.15 = f32[5248]{0:T(1024)S(1)} all-reduce(f32[5248]{0:T(1024)S(1)} %pad_maximum_fusion), channel_id=1, replica_groups=mesh['gen'=4,'learn'=32] {'gen','learn'}, use_global_device_ids=true, to_apply=%region_10.11 | all-reduce | flops 5248 | bytes 41984 | tf_op jit(solution)/shard_map/psum | solution.py:20
  218.8 0.6 slice.8
  219.4 0.5 slice.9
  219.9 28.3 %all-reduce.2.cloned.1.call-done = f32[1280,1024]{1,0:T(8,128)} async-done(((f32[1280,1024]{1,0:T(8,128)}), f32[1280,1024]{1,0:T(8,128)}) %all-reduce.2.cloned.1.call-update) | async-done | bytes 5242896 | tf_op jit(solution)/shard_map/psum | solution.py:103
  248.2 5.3 %copy.39 = bf16[512,5120]{1,0:T(8,128)(2,1)} copy(bf16[512,5120]{1,0:T(8,128)(2,1)} %bitcast.2) | data formatting | bytes 10485760
  253.6 2.4 copy.40
  (44 shorter events, 0.7 us)
Async XLA Ops:
  7.2 83.2 %all-gather.2.cloned.1.call-start = ((), (), s32[]{:S(2)}) async-start(), calls=%async_computation.2 | async-start | bytes 2621440 | tf_op jit(solution)/shard_map/all_gather | solution.py:99
  12.1 6.6 %copy-start.1 = (bf16[256,5120]{1,0:T(8,128)(2,1)}, bf16[256,5120]{1,0:T(8,128)(2,1)S(1)}, u32[]{:S(2)}) copy-start(bf16[256,5120]{1,0:T(8,128)(2,1)S(1)} %fusion.4) | copy-start | bytes 7864324
  12.1 6.8 %copy-start.10 = (s32[32]{0:T(128)S(1)}, s32[32]{0:T(128)}, u32[]{:S(2)}) copy-start(s32[32]{0:T(128)} %param.13) | copy-start | bytes 388
  12.1 6.8 %copy-start.9 = (s32[32]{0:T(128)S(1)}, s32[32]{0:T(128)}, u32[]{:S(2)}) copy-start(s32[32]{0:T(128)} %param.12) | copy-start | bytes 388
  12.1 7.0 %copy-start.8 = (f32[256]{0:T(256)S(1)}, f32[256]{0:T(256)}, u32[]{:S(2)}) copy-start(f32[256]{0:T(256)} %param.11) | copy-start | bytes 3076
  12.1 7.0 %copy-start.4 = (bf16[256,1024]{1,0:T(8,128)(2,1)S(1)}, bf16[256,1024]{1,0:T(8,128)(2,1)}, u32[]{:S(2)}) copy-start(bf16[256,1024]{1,0:T(8,128)(2,1)} %param.10) | copy-start | bytes 1572868
  18.7 0.8 copy-start.6
  23.7 9.4 %copy-start = (bf16[256,5120]{1,0:T(8,128)(2,1)S(1)}, bf16[256,5120]{1,0:T(8,128)(2,1)}, u32[]{:S(2)}) copy-start(bf16[256,5120]{1,0:T(8,128)(2,1)} %param.9) | copy-start | bytes 7864324
  23.8 9.4 %copy-start.3 = (bf16[256,1024]{1,0:T(8,128)(2,1)S(1)}, bf16[256,1024]{1,0:T(8,128)(2,1)}, u32[]{:S(2)}) copy-start(bf16[256,1024]{1,0:T(8,128)(2,1)} %get-tuple-element.9) | copy-start | bytes 1572868
  23.8 9.4 %copy-start.5 = (f32[5120]{0:T(1024)S(1)}, f32[5120]{0:T(1024)}, u32[]{:S(2)}) copy-start(f32[5120]{0:T(1024)} %param.16) | copy-start | bytes 61444
  27.3 54.1 %all-to-all-start.1 = ((bf16[256,4,1280]{2,0,1:T(8,128)(2,1)}), bf16[256,4,1280]{2,0,1:T(8,128)(2,1)}, u32[]{:S(2)}, u32[]{:S(2)}) async-start(bf16[256,4,1280]{2,0,1:T(8,128)(2,1)} %bitcast.44), calls=%async_computation.1 | async-start | bytes 5242880 | tf_op jit(solution)/shard_map/all_to_all | solution.py:96
  42.7 3.2 %copy-start.7 = (s32[32,1]{0,1:T(1,128)S(1)}, s32[32,1]{0,1:T(1,128)}, u32[]{:S(2)}) copy-start(s32[32,1]{0,1:T(1,128)} %param.14) | copy-start | bytes 388
  81.5 138.5 %all-to-all-start = ((bf16[32,16,5120]{2,1,0:T(8,128)(2,1)}), bf16[32,16,5120]{2,1,0:T(8,128)(2,1)}, u32[]{:S(2)}, u32[]{:S(2)}) async-start(bf16[32,16,5120]{2,1,0:T(8,128)(2,1)} %all_to_all.19), calls=%async_computation | async-start | bytes 10485760 | tf_op jit(solution)/shard_map/all_to_all | solution.py:86
  90.3 157.9 %all-reduce.2.cloned.1.call-start = ((), (), s32[]{:S(2)}) async-start(), calls=%async_computation.3 | async-start | bytes 10485760 | tf_op jit(solution)/shard_map/psum | solution.py:103
  248.2 5.3 %copy-start.2 = (f32[1280,1024]{1,0:T(8,128)S(1)}, f32[1280,1024]{1,0:T(8,128)}, u32[]{:S(2)}) copy-start(f32[1280,1024]{1,0:T(8,128)} %all-reduce.2.cloned.1.call-done) | copy-start | bytes 15728644
Sparse Core Ops, SparseCore 0:
  23.9 59.1 all-gather.1
  98.2 149.9 all-reduce.1
where the time goes:
time: 263 us
  blocking collectives  121 us (46%)
  waiting for transfers between devices  51.6 us (20%)
  local copies, waits for them, and re-layouts  25.7 us (10%)
  matrix products  24.5 us (9%)
  starting transfers between devices  14.8 us (6%)
  between operations  14.3 us (5%)
  other arithmetic  11.1 us (4%)
    psum x1, blocking collectives, packed_total(): so_far = lax.psum(jnp.concatenate([a.ravel() for a in arrays]), axis)  121 us
    psum x1, waiting for transfers between devices, body(): w_grad = lax.psum(partial_rows, 'learn')  28.3 us
    all_to_all x1, waiting for transfers between devices, body(): lax.all_to_all(sliced, 'gen', split_axis=1, concat_axis=0, tiled=True)  23.3 us
    all_to_all x1, starting transfers between devices, body(): lax.all_to_all(spread.astype(jnp.bfloat16).reshape(SLOTS * TILE, feature_...  8.84 us
    unnamed x26, local copies, waits for them, and re-layouts  8.15 us
    all_to_all x1, local copies, waits for them, and re-layouts, body(): lax.all_to_all(spread.astype(jnp.bfloat16).reshape(SLOTS * TILE, feature_...  8.08 us
    dot_general x1, matrix products, body(): lax.dot_general(arrived_rows, gathered_keys, (((0,), (0,)), ((), ())), pr...  7.66 us
    dot_general x1, matrix products, layer_pass(): jnp.dot(h_rows, w_key, preferred_element_type=jnp.float32)  6.55 us
  transfers between devices with their start and end apart: 4, of which 2 were waited for; matrix products, arithmetic and copies ran while one was open for 11% of the time, Pallas kernels for 0%

commit v1 on v0

v1 whole, which is shorter than its diff:
```python
import functools

import jax
import jax.numpy as jnp
from jax import lax
from jax.experimental import pallas as pl
from jax.experimental.pallas import tpu as pltpu
from jax.sharding import PartitionSpec as P

MESH = pl.DeviceIdType.MESH
F32 = jnp.float32
BF16 = jnp.bfloat16

D = 5120
KD = 1024
HD = 128
ROWS = 256
TILE = 8
SR = 512
PAIR = 16
PIECE = D // 8
EPS = 1e-06

OTHERS = (
    (1, 0), (3, 0), (0, 1), (0, 3), (1, 1), (3, 3), (1, 3), (3, 1),
    (2, 0), (0, 2), (2, 1), (1, 2), (2, 3), (3, 2), (2, 2),
)
ORDER = ((0, 0, 1),) + tuple((a, b, c) for (a, b) in OTHERS for c in range(2))
ZPEERS = ((0, 1), (1, 0), (3, 0), (1, 1), (3, 1), (2, 0), (2, 1))


def ds(start, size, mult=None):
    return pl.ds(start if mult is None else pl.multiple_of(start, mult), size)


def kernel(
    hid, cot, imp, blen, ver, dest, w, gain, kgain,
    slots_out, w_out, g_out,
    x_v, w_v, cot_v, inv_v, cw_v, h_v, gk_v, msum_v, place_v, slots_v, hbuf, gkbuf, acc,
    rs1s, rs1r, rs2s, rs2r, wbuf, gbuf1, gbuf2, gbuf3,
    in_sem, w_sem, own_sem, h_ss, h_rs, k_ss, k_rs, rel_ss, s_ss, s_rs,
    r1_ss, r1_rs, r2_ss, r2_rs, ab_ss, ab_rs, aa_ss, aa_rs, ac_ss, ac_rs,
    g1_ss, g1_rs, g2_ss, g2_rs, g3_ss, g3_rs,
):
    g = lax.axis_index("gen")
    l = lax.axis_index("learn")
    x = l // 8
    y = (l // 2) % 4
    c = l % 2
    a = x + c * (y - x)
    b = y + c * (x - y)
    me = g * 2 + c

    def plane(px, py, pc):
        return (g, px * 8 + py * 2 + pc)

    def a_dev(na):
        return plane(x + (1 - c) * (na - x), y + c * (na - y), c)

    def b_dev(nb):
        return plane(x + c * (nb - x), y + (1 - c) * (nb - y), c)

    def z_dev(q, pc):
        return (q, x * 8 + y * 2 + pc)

    def remote(src, dst, ss, rs, dev):
        return pltpu.make_async_remote_copy(src, dst, ss, rs, device_id=dev, device_id_type=MESH)

    for i in range(4):
        rows = ds(i * 64, 64)
        pltpu.make_async_copy(hid.at[rows], x_v.at[rows], in_sem.at[i]).start()
    pltpu.make_async_copy(cot, cot_v, in_sem.at[4]).start()
    for n in range(4):
        cols = ds(n * 256, 256)
        pltpu.make_async_copy(w.at[:, cols], w_v.at[:, cols], w_sem.at[n]).start()

    barrier = pltpu.get_barrier_semaphore()

    @pl.loop(1, 32)
    def _(i):
        pl.semaphore_signal(barrier, inc=1, device_id=(g, lax.rem(l + i, 32)), device_id_type=MESH)

    for dz, dc in ZPEERS[1:]:
        pl.semaphore_signal(
            barrier, inc=1, device_id=z_dev(lax.rem(g + dz, 4), lax.rem(c + dc, 2)), device_id_type=MESH
        )

    r256 = lax.broadcasted_iota(jnp.int32, (ROWS, ROWS), 0)
    j256 = lax.broadcasted_iota(jnp.int32, (ROWS, ROWS), 1)
    imp_col = jnp.sum(jnp.where(r256 == j256, imp[...], 0.0), axis=1, keepdims=True)
    r32 = lax.broadcasted_iota(jnp.int32, (ROWS, 32), 0)
    j32 = lax.broadcasted_iota(jnp.int32, (ROWS, 32), 1)
    of_block = (r32 >> 3) == j32
    len_col = jnp.sum(jnp.where(of_block, blen[...].astype(F32), 0.0), axis=1, keepdims=True)
    ver_col = jnp.sum(jnp.where(of_block, ver[...].astype(F32), 0.0), axis=1, keepdims=True)
    row_col = (lax.broadcasted_iota(jnp.int32, (ROWS, 1), 0) & 7).astype(F32)
    inside = jnp.where(row_col < len_col, 1.0, 0.0)
    age = 3.0 - ver_col
    decay = jnp.where(age == 0.0, 1.0, jnp.where(age == 1.0, 0.5, jnp.where(age == 2.0, 0.25, 0.125)))
    cw_v[...] = jnp.broadcast_to(jnp.minimum(imp_col, 2.0) * (decay * inside), (ROWS, HD))

    blk = lax.broadcasted_iota(jnp.int32, (32, ROWS), 0)
    row_blk = lax.broadcasted_iota(jnp.int32, (32, ROWS), 1) >> 3
    dest_col = dest[...].astype(F32)
    dest_row = jnp.sum(jnp.where(blk == row_blk, dest_col, 0.0), axis=0, keepdims=True)
    rank_row = jnp.sum(jnp.where((blk < row_blk) & (dest_col == dest_row), 1.0, 0.0), axis=0, keepdims=True)
    target = dest_row * 2.0 + rank_row
    srow = lax.broadcasted_iota(jnp.int32, (SR, ROWS), 0)
    scol = lax.broadcasted_iota(jnp.int32, (SR, ROWS), 1)
    hit = ((srow >> 3).astype(F32) == target) & ((srow & 7) == (scol & 7))
    place_v[...] = jnp.where(hit, 1.0, 0.0).astype(BF16)

    @pl.loop(0, 4)
    def _(i):
        big = ds(i * 64, 64, 64)
        pltpu.make_async_copy(hid.at[big], x_v.at[big], in_sem.at[i]).wait()

        @pl.loop(0, 4)
        def _(k):
            rows = ds(i * 64 + k * 16, 16, 16)
            total = jnp.zeros((16, HD), F32)
            for f in range(D // HD):
                xf = x_v[rows, f * HD : (f + 1) * HD].astype(F32)
                total = total + xf * xf
            inv = lax.rsqrt(jnp.sum(total, axis=1, keepdims=True) * (1.0 / D) + EPS)
            inv = jnp.broadcast_to(inv, (16, HD))
            inv_v[rows, :] = inv
            for f in range(D // HD):
                cols = slice(f * HD, (f + 1) * HD)
                h_v[rows, cols] = (x_v[rows, cols].astype(F32) * inv * gain[:, cols]).astype(BF16)

    pl.semaphore_wait(barrier, 31 + 6)

    h_copies = []
    for i, (dz, dc) in enumerate(ZPEERS):
        q, pc = lax.rem(g + dz, 4), lax.rem(c + dc, 2)
        piece = h_v.at[:, ds((q * 2 + pc) * PIECE, PIECE, 128)]
        copy = remote(piece, hbuf.at[me], h_ss.at[i], h_rs.at[me], z_dev(q, pc))
        copy.start()
        h_copies.append(copy)

    pltpu.make_async_copy(cot, cot_v, in_sem.at[4]).wait()
    msum_v[...] = jnp.zeros((ROWS, HD), F32)

    def key_tile(n, kg):
        cols = ds(n * 256, 256, 256)
        pltpu.make_async_copy(w.at[:, cols], w_v.at[:, cols], w_sem.at[n]).wait()
        keys = jnp.dot(h_v[...], w_v[:, cols], preferred_element_type=F32)
        for s in range(2):
            k = keys[:, s * HD : (s + 1) * HD]
            head = ds(n * 256 + s * HD, HD, HD)
            scale = lax.rsqrt(jnp.sum(k * k, axis=1, keepdims=True) * (1.0 / HD) + EPS)
            up = (cot_v[:, head].astype(F32) * cw_v[...]).astype(BF16).astype(F32)
            kg = kg + jnp.sum(up * k * scale, axis=0, keepdims=True)
            u = up * kgain[...]
            mean = jnp.sum(u * k, axis=1, keepdims=True) * (1.0 / HD)
            gk = (scale * u - k * (scale * scale * scale) * mean).astype(BF16)
            gk_v[:, head] = gk
            msum_v[...] += gk.astype(F32) * k
        return kg

    kg = lax.fori_loop(0, 4, key_tile, jnp.zeros((1, HD), F32))
    gbuf1[me, :, D:] = kg

    k_copies = []
    for i, (dz, dc) in enumerate(((0, 1), (1, 0), (3, 0), (2, 0))):
        q, pc = lax.rem(g + dz, 4), lax.rem(c + dc, 2)
        copy = remote(gk_v, gkbuf.at[me], k_ss.at[i], k_rs.at[me], z_dev(q, pc))
        copy.start()
        k_copies.append(copy)

    mean = jnp.sum(msum_v[...], axis=1, keepdims=True) * (1.0 / D)
    msum_v[...] = jnp.broadcast_to(mean, (ROWS, HD))

    @pl.loop(0, 4)
    def _(q):
        @pl.loop(0, 5)
        def _(s):
            f = pl.multiple_of(q * 1280 + s * 256, 256)
            cols = pl.ds(f, 256)
            grad_h = lax.dot_general(
                gk_v[...], w_v[cols, :], (((1,), (1,)), ((), ())), preferred_element_type=F32
            )
            inv = jnp.concatenate([inv_v[...]] * 2, axis=1)
            mean = jnp.concatenate([msum_v[...]] * 2, axis=1)
            normed = x_v[:, cols].astype(F32) * inv
            gbuf1[me, :, cols] = jnp.sum(grad_h * normed, axis=0, keepdims=True)
            grad_in = (inv * (grad_h * gain[:, cols] - normed * mean)).astype(BF16)
            slots_v[:, cols] = jnp.dot(place_v[...], grad_in, preferred_element_type=F32).astype(BF16)

        quarter = ds(q * 1280, 1280, 1280)
        for dx, dy, dc in ORDER:
            dev = plane(lax.rem(x + dx, 4), lax.rem(y + dy, 4), lax.rem(c + dc, 2))
            remote(
                slots_v.at[ds(dev[1] * PAIR, PAIR, PAIR), quarter],
                slots_out.at[ds(l * PAIR, PAIR, PAIR), quarter],
                s_ss, s_rs, dev,
            ).start()

    mine = ds(l * PAIR, PAIR, PAIR)
    own = pltpu.make_async_copy(slots_v.at[mine], slots_out.at[mine], own_sem)
    own.start()

    def broadcast(buf, place, peers, ss, rs):
        copies = []
        for i, dev in enumerate(peers):
            copy = remote(buf.at[place], buf.at[place], ss.at[i], rs.at[place], dev)
            copy.start()
            copies.append(copy)
        return copies

    def arrived(buf, place, rs):
        remote(buf.at[place], buf.at[place], rs.at[place], rs.at[place], (g, l)).wait_recv()

    g_copies = broadcast(
        gbuf1, me, [z_dev(lax.rem(g + dz, 4), lax.rem(c + dc, 2)) for dz, dc in ZPEERS], g1_ss, g1_rs
    )

    def add(hs, gks, first=False):
        part = lax.dot_general(hs, gks, (((0,), (0,)), ((), ())), preferred_element_type=F32)
        if first:
            acc[...] = part
        else:
            acc[...] += part

    add(h_v[:, ds(me * PIECE, PIECE, 128)], gk_v[...], True)
    partner = z_dev(g, 1 - c)
    other = g * 2 + 1 - c
    arrived(hbuf, other, h_rs)
    arrived(gkbuf, other, k_rs)
    add(hbuf[other], gkbuf[other])

    for dz, dc in ZPEERS:
        arrived(gbuf1, lax.rem(g + dz, 4) * 2 + lax.rem(c + dc, 2), g1_rs)
    total = gbuf1[0]
    for i in range(1, 8):
        total = total + gbuf1[i]
    gbuf2[x] = total
    g_copies += broadcast(gbuf2, x, [plane(lax.rem(x + d, 4), y, c) for d in (1, 3, 2)], g2_ss, g2_rs)

    rel_copies = []
    for i, dz in enumerate((1, 3, 2)):
        q = lax.rem(g + dz, 4)
        same, cross = q * 2 + c, q * 2 + 1 - c
        arrived(gkbuf, same, k_rs)
        copy = remote(gkbuf.at[same], gkbuf.at[same], rel_ss.at[i], k_rs.at[same], partner)
        copy.start()
        rel_copies.append(copy)
        arrived(hbuf, same, h_rs)
        add(hbuf[same], gkbuf[same])
        arrived(hbuf, cross, h_rs)
        arrived(gkbuf, cross, k_rs)
        add(hbuf[cross], gkbuf[cross])

    rs1s[...] = acc[...].astype(BF16)
    w_copies = []
    for i, d in enumerate((1, 3, 2)):
        na = lax.rem(a + d, 4)
        copy = remote(rs1s.at[ds(na * 160, 160, 16)], rs1r.at[a], r1_ss.at[i], r1_rs.at[a], a_dev(na))
        copy.start()
        w_copies.append(copy)

    for d in (1, 3, 2):
        arrived(gbuf2, lax.rem(x + d, 4), g2_rs)
    gbuf3[y] = (gbuf2[0] + gbuf2[1]) + (gbuf2[2] + gbuf2[3])
    g_copies += broadcast(gbuf3, y, [plane(x, lax.rem(y + d, 4), c) for d in (1, 3, 2)], g3_ss, g3_rs)

    held = acc.at[ds(a * 160, 160, 8)]
    for d in (1, 3, 2):
        na = lax.rem(a + d, 4)
        arrived(rs1r, na, r1_rs)
        held[...] += rs1r[na].astype(F32)
    for n in range(4):
        rs2s[n] = held[:, n * 256 : (n + 1) * 256].astype(BF16)
    for i, d in enumerate((1, 3, 2)):
        nb = lax.rem(b + d, 4)
        copy = remote(rs2s.at[nb], rs2r.at[b], r2_ss.at[i], r2_rs.at[b], b_dev(nb))
        copy.start()
        w_copies.append(copy)
    total = held[:, ds(b * 256, 256, 256)]
    for d in (1, 3, 2):
        nb = lax.rem(b + d, 4)
        arrived(rs2r, nb, r2_rs)
        total = total + rs2r[nb].astype(F32)

    def rows_of(na, pc):
        return ds(pc * 640 + na * 160, 160, 16)

    def block(na, nb):
        return wbuf.at[rows_of(na, c), ds(nb * 256, 256, 256)]

    wbuf[rows_of(a, c), ds(b * 256, 256, 256)] = total.astype(BF16)
    for i, d in enumerate((1, 3, 2)):
        copy = remote(block(a, b), block(a, b), ab_ss.at[i], ab_rs.at[b], b_dev(lax.rem(b + d, 4)))
        copy.start()
        w_copies.append(copy)
    for d in (1, 3, 2):
        nb = lax.rem(b + d, 4)
        remote(block(a, nb), block(a, nb), ab_rs.at[nb], ab_rs.at[nb], (g, l)).wait_recv()
    band = wbuf.at[rows_of(a, c)]
    for i, d in enumerate((1, 3, 2)):
        copy = remote(band, band, aa_ss.at[i], aa_rs.at[a], a_dev(lax.rem(a + d, 4)))
        copy.start()
        w_copies.append(copy)
    copy = remote(band, band, ac_ss.at[0], ac_rs.at[a], partner)
    copy.start()
    w_copies.append(copy)
    for i, d in enumerate((1, 3, 2)):
        na = lax.rem(a + d, 4)
        band = wbuf.at[rows_of(na, c)]
        remote(band, band, aa_rs.at[na], aa_rs.at[na], (g, l)).wait_recv()
        copy = remote(band, band, ac_ss.at[i + 1], ac_rs.at[na], partner)
        copy.start()
        w_copies.append(copy)
    for n in range(4):
        band = wbuf.at[rows_of(n, 1 - c)]
        remote(band, band, ac_rs.at[n], ac_rs.at[n], (g, l)).wait_recv()
    out = pltpu.make_async_copy(wbuf, w_out, in_sem.at[0])
    out.start()

    for d in (1, 3, 2):
        arrived(gbuf3, lax.rem(y + d, 4), g3_rs)
    g_out[...] = (gbuf3[0] + gbuf3[1]) + (gbuf3[2] + gbuf3[3])

    for copy in h_copies + k_copies + g_copies + rel_copies + w_copies:
        copy.wait_send()
    own.wait()
    everyone = remote(slots_v.at[ds(0, 31 * PAIR)], slots_out.at[ds(0, 31 * PAIR)], s_ss, s_rs, (g, l))
    everyone.wait_send()
    everyone.wait_recv()
    out.wait()


def body(hidden, cotangent, importance, block_len, version, destination, w_key, in_gain, key_gain):
    dma = pltpu.SemaphoreType.DMA
    vmem = pl.BlockSpec(memory_space=pltpu.VMEM)
    hbm = pl.BlockSpec(memory_space=pl.ANY)
    slots, w_rows, gains = pl.pallas_call(
        kernel,
        name="grad_step",
        out_shape=(
            jax.ShapeDtypeStruct((SR, D), BF16),
            jax.ShapeDtypeStruct((D // 4, KD), BF16),
            jax.ShapeDtypeStruct((1, D + HD), F32),
        ),
        in_specs=[hbm, hbm, vmem, vmem, vmem, vmem, hbm, vmem, vmem],
        out_specs=(hbm, hbm, vmem),
        scratch_shapes=[
            pltpu.VMEM((ROWS, D), BF16),
            pltpu.VMEM((D, KD), BF16),
            pltpu.VMEM((ROWS, KD), BF16),
            pltpu.VMEM((ROWS, HD), F32),
            pltpu.VMEM((ROWS, HD), F32),
            pltpu.VMEM((ROWS, D), BF16),
            pltpu.VMEM((ROWS, KD), BF16),
            pltpu.VMEM((ROWS, HD), F32),
            pltpu.VMEM((SR, ROWS), BF16),
            pltpu.VMEM((SR, D), BF16),
            pltpu.VMEM((8, ROWS, PIECE), BF16),
            pltpu.VMEM((8, ROWS, KD), BF16),
            pltpu.VMEM((PIECE, KD), F32),
            pltpu.VMEM((PIECE, KD), BF16),
            pltpu.VMEM((4, 160, KD), BF16),
            pltpu.VMEM((4, 160, 256), BF16),
            pltpu.VMEM((4, 160, 256), BF16),
            pltpu.VMEM((D // 4, KD), BF16),
            pltpu.VMEM((8, 1, D + HD), F32),
            pltpu.VMEM((4, 1, D + HD), F32),
            pltpu.VMEM((4, 1, D + HD), F32),
            dma((5,)), dma((4,)), dma(()),
            dma((7,)), dma((8,)), dma((4,)), dma((8,)), dma((3,)), dma(()), dma(()),
            dma((3,)), dma((4,)), dma((3,)), dma((4,)),
            dma((3,)), dma((4,)), dma((3,)), dma((4,)), dma((4,)), dma((4,)),
            dma((7,)), dma((8,)), dma((3,)), dma((4,)), dma((3,)), dma((4,)),
        ],
        compiler_params=pltpu.CompilerParams(
            collective_id=0, has_side_effects=True, vmem_limit_bytes=60 * 1024 * 1024
        ),
    )(
        hidden, cotangent, importance.reshape(1, ROWS), block_len.reshape(1, 32),
        version.reshape(1, 32), destination, w_key, in_gain.reshape(1, D), key_gain.reshape(1, HD),
    )
    return slots, w_rows.astype(F32), gains[0, :D], gains[0, D:]


def solution(mesh):
    return jax.shard_map(
        body,
        mesh=mesh,
        in_specs=(
            P(("gen", "learn"), None),
            P(("gen", "learn"), None),
            P(("gen", "learn")),
            P(("gen", "learn")),
            P(("gen", "learn")),
            P(("gen", "learn"), None),
            P(),
            P(),
            P(),
        ),
        out_specs=(P(("gen", "learn"), None), P("gen", None), P(), P()),
        check_vma=False,
    )
```

time: 263 us -> 126 us (0.48)
  the two profiles are of different devices: /device:TPU:1 before, /device:TPU:5 now
where the time goes in v1:
time: 126 us; the launch traced here: 125 us
  Pallas kernels  113 us (90%)
  local copies, waits for them, and re-layouts  6.59 us (5%)
  other arithmetic  4.75 us (4%)
    pallas_call x1, Pallas kernels, body(): pl.pallas_call(kernel, name='grad_step', out_shape=(jax.ShapeDtypeStruct(...  113 us
    convert_element_type x1, other arithmetic, body(): return (slots, w_rows.astype(F32), gains[0, :D], gains[0, D:])  4.75 us
    unnamed x4, local copies, waits for them, and re-layouts  3.7 us

profile of v1, /device:TPU:5, one launch (start us, length us, event | category | flops | bytes accessed | tf_op | source)
XLA Modules:
  0.0 125.4 jit_solution(17512156357965197038)
XLA Ops:
  0.6 1.3 %copy.13.dest = s32[32,1]{1,0:T(8,128)} copy(s32[32,1]{0,1:T(1,128)} %param.14) | data formatting | bytes 256 | tf_op args[5]
  2.0 113.5 %grad_step.1 = (bf16[512,5120]{1,0:T(8,128)(2,1)}, bf16[1280,1024]{1,0:T(8,128)(2,1)}, f32[1,5248]{1,0:T(1,128)}) custom-call(bf16[256,5120]{1,0:T(8,128)(2,1)} %hid.1, bf16[256,1024]{1,0:T(8,128)(2,1)} %cot.1, f32[1,256]{1,0:T(1,128)} %bitcast.10, s32[1,32]{1,0:T(1,128)} %bitcast.11, s32[1,32]{1,0:T(1,128)} %bitcast.12, s32[32,1]{1,0:T(8,128)} %copy.13.dest, ...), custom_call_target="tpu_custom_call" | custom-call | tf_op jit(solution)/shard_map/grad_step/pallas_call | solution.py:338
  115.4 0.0 copy-start
  115.5 1.3 %slice_bitcast_fusion = f32[128]{0:T(128)} fusion(f32[1,5248]{1,0:T(1,128)} %get-tuple-element.9), kind=kLoop, calls=%fused_computation | loop fusion | bytes 1024 | tf_op jit(solution)/shard_map/squeeze | solution.py:383
  116.8 1.6 %slice.6 = f32[1,5120]{1,0:T(1,128)} slice(f32[1,5248]{1,0:T(1,128)} %get-tuple-element.9), slice={[0:1], [0:5120]} | slice | bytes 40960 | tf_op jit(solution)/shard_map/slice | solution.py:383
  118.3 4.7 %convert_element_type.3 = f32[1280,1024]{1,0:T(8,128)} convert(bf16[1280,1024]{1,0:T(8,128)(2,1)} %get-tuple-element.8) | non-fusion elementwise | flops 1310720 | bytes 7864320 | tf_op jit(solution)/shard_map/convert_element_type | solution.py:383
  123.1 0.0 copy-done
  123.1 2.4 %copy.15 = bf16[512,5120]{1,0:T(8,128)(2,1)} copy(bf16[512,5120]{1,0:T(8,128)(2,1)S(1)} %copy-done) | data formatting | bytes 10485760
Async XLA Ops:
  115.4 7.6 %copy-start = (bf16[512,5120]{1,0:T(8,128)(2,1)S(1)}, bf16[512,5120]{1,0:T(8,128)(2,1)}, u32[]{:S(2)}) copy-start(bf16[512,5120]{1,0:T(8,128)(2,1)} %get-tuple-element.14) | copy-start | bytes 15728644

commit v2 on v1

v2 whole, which is shorter than its diff:
```python
import functools

import jax
import jax.numpy as jnp
from jax import lax
from jax.experimental import pallas as pl
from jax.experimental.pallas import tpu as pltpu
from jax.sharding import PartitionSpec as P

MESH = pl.DeviceIdType.MESH
F32 = jnp.float32
BF16 = jnp.bfloat16

D = 5120
KD = 1024
HD = 128
ROWS = 256
TILE = 8
SR = 512
PAIR = 16
PIECE = D // 8
FC = 128
NC = PIECE // FC
TW = 256
EPS = 1e-06

OTHERS = (
    (1, 0), (3, 0), (0, 1), (0, 3), (1, 1), (3, 3), (1, 3), (3, 1),
    (2, 0), (0, 2), (2, 1), (1, 2), (2, 3), (3, 2), (2, 2),
)
ORDER = ((0, 0, 1),) + tuple((a, b, c) for (a, b) in OTHERS for c in range(2))
ZPEERS = ((0, 1), (1, 0), (3, 0), (1, 1), (3, 1), (2, 0), (2, 1))


def ds(start, size, mult=None):
    return pl.ds(start if mult is None else pl.multiple_of(start, mult), size)


def kernel(
    hid, cot, imp, blen, ver, dest, w, gain, kgain,
    slots_out, w_out, g_out, kg_out,
    x_v, w_v, cot_v, inv_v, cw_v, h_v, msum_v, place_v, slots_v, hbuf, gkbuf, acc, tot_v,
    rs1s, rs1r, rs2s, rs2r, wbuf, gbuf1, gbuf2, gbuf3,
    in_sem, w_sem, own_sem, h_ss, h_rs, k_ss, k_rs, rel_ss, s_ss, s_rs,
    r1_ss, r1_rs, r2_ss, r2_rs, ab_ss, ab_rs, aa_ss, aa_rs, ac_ss, ac_rs,
    g1_ss, g1_rs, g2_ss, g2_rs, g3_ss, g3_rs,
):
    g = lax.axis_index("gen")
    l = lax.axis_index("learn")
    x = l // 8
    y = (l // 2) % 4
    c = l % 2
    a = x + c * (y - x)
    b = y + c * (x - y)
    me = g * 2 + c

    def plane(px, py, pc):
        return (g, px * 8 + py * 2 + pc)

    def a_dev(na):
        return plane(x + (1 - c) * (na - x), y + c * (na - y), c)

    def b_dev(nb):
        return plane(x + c * (nb - x), y + (1 - c) * (nb - y), c)

    def z_dev(q, pc):
        return (q, x * 8 + y * 2 + pc)

    def remote(src, dst, ss, rs, dev):
        return pltpu.make_async_remote_copy(src, dst, ss, rs, device_id=dev, device_id_type=MESH)

    for i in range(4):
        rows = ds(i * 64, 64)
        pltpu.make_async_copy(hid.at[rows], x_v.at[rows], in_sem.at[i]).start()
    for n in range(4):
        cols = ds(n * 256, 256)
        pltpu.make_async_copy(w.at[:, cols], w_v.at[:, cols], w_sem.at[n]).start()
    pltpu.make_async_copy(cot, cot_v, in_sem.at[4]).start()

    barrier = pltpu.get_barrier_semaphore()

    @pl.loop(1, 32)
    def _(i):
        pl.semaphore_signal(barrier, inc=1, device_id=(g, lax.rem(l + i, 32)), device_id_type=MESH)

    for dz, dc in ZPEERS[1:]:
        pl.semaphore_signal(
            barrier, inc=1, device_id=z_dev(lax.rem(g + dz, 4), lax.rem(c + dc, 2)), device_id_type=MESH
        )

    r256 = lax.broadcasted_iota(jnp.int32, (ROWS, ROWS), 0)
    j256 = lax.broadcasted_iota(jnp.int32, (ROWS, ROWS), 1)
    imp_col = jnp.sum(jnp.where(r256 == j256, imp[...], 0.0), axis=1, keepdims=True)
    r32 = lax.broadcasted_iota(jnp.int32, (ROWS, 32), 0)
    j32 = lax.broadcasted_iota(jnp.int32, (ROWS, 32), 1)
    of_block = (r32 >> 3) == j32
    len_col = jnp.sum(jnp.where(of_block, blen[...].astype(F32), 0.0), axis=1, keepdims=True)
    ver_col = jnp.sum(jnp.where(of_block, ver[...].astype(F32), 0.0), axis=1, keepdims=True)
    row_col = (lax.broadcasted_iota(jnp.int32, (ROWS, 1), 0) & 7).astype(F32)
    inside = jnp.where(row_col < len_col, 1.0, 0.0)
    age = 3.0 - ver_col
    decay = jnp.where(age == 0.0, 1.0, jnp.where(age == 1.0, 0.5, jnp.where(age == 2.0, 0.25, 0.125)))
    cw_v[...] = jnp.broadcast_to(jnp.minimum(imp_col, 2.0) * (decay * inside), (ROWS, HD))

    b32 = lax.broadcasted_iota(jnp.int32, (32, 32), 0)
    e32 = lax.broadcasted_iota(jnp.int32, (32, 32), 1)
    dest_col = jnp.sum(jnp.where(b32 == e32, dest[...].astype(F32), 0.0), axis=1, keepdims=True)
    blk = lax.broadcasted_iota(jnp.int32, (32, ROWS), 0)
    row_blk = lax.broadcasted_iota(jnp.int32, (32, ROWS), 1) >> 3
    dest_row = jnp.sum(jnp.where(blk == row_blk, dest_col, 0.0), axis=0, keepdims=True)
    rank_row = jnp.sum(jnp.where((blk < row_blk) & (dest_col == dest_row), 1.0, 0.0), axis=0, keepdims=True)
    target = dest_row * 2.0 + rank_row
    srow = lax.broadcasted_iota(jnp.int32, (SR, ROWS), 0)
    scol = lax.broadcasted_iota(jnp.int32, (SR, ROWS), 1)
    hit = ((srow >> 3).astype(F32) == target) & ((srow & 7) == (scol & 7))
    place_v[...] = jnp.where(hit, 1.0, 0.0).astype(BF16)

    @pl.loop(0, 4)
    def _(i):
        big = ds(i * 64, 64, 64)
        pltpu.make_async_copy(hid.at[big], x_v.at[big], in_sem.at[i]).wait()
        invs = []
        for k in range(4):
            rows = ds(i * 64 + k * 16, 16, 16)
            total = jnp.zeros((16, HD), F32)
            for f in range(D // HD):
                xf = x_v[rows, f * HD : (f + 1) * HD].astype(F32)
                total = total + xf * xf
            inv = lax.rsqrt(jnp.sum(total, axis=1, keepdims=True) * (1.0 / D) + EPS)
            inv = jnp.broadcast_to(inv, (16, HD))
            inv_v[rows, :] = inv
            invs.append(inv)
        for k in range(4):
            rows = ds(i * 64 + k * 16, 16, 16)
            for f in range(D // HD):
                cols = slice(f * HD, (f + 1) * HD)
                h_v[rows, cols] = (x_v[rows, cols].astype(F32) * invs[k] * gain[:, cols]).astype(BF16)

    pl.semaphore_wait(barrier, 31 + 6)

    def mine(ref):
        return ref.at[ds(me * ROWS, ROWS, ROWS)]

    def send_h(k):
        for dz, dc in ZPEERS:
            q, pc = lax.rem(g + dz, 4), lax.rem(c + dc, 2)
            piece = h_v.at[:, ds((q * 2 + pc) * PIECE + k * FC, FC, FC)]
            remote(piece, mine(hbuf.at[k]), h_ss, h_rs.at[k, me], z_dev(q, pc)).start()

    send_h(0)
    for k in range(NC):
        hbuf[k, ds(me * ROWS, ROWS, ROWS), :] = h_v[:, ds(me * PIECE + k * FC, FC, FC)]

    pltpu.make_async_copy(cot, cot_v, in_sem.at[4]).wait()
    for n in range(4):
        cols = ds(n * 256, 256)
        pltpu.make_async_copy(w.at[:, cols], w_v.at[:, cols], w_sem.at[n]).wait()
    kg = jnp.zeros((1, HD), F32)
    for n in range(4):
        keys = jnp.dot(h_v[...], w_v[:, n * 256 : (n + 1) * 256], preferred_element_type=F32)
        for s in range(2):
            k = keys[:, s * HD : (s + 1) * HD]
            head = slice(n * 256 + s * HD, n * 256 + s * HD + HD)
            scale = lax.rsqrt(jnp.sum(k * k, axis=1, keepdims=True) * (1.0 / HD) + EPS)
            up = (cot_v[:, head].astype(F32) * cw_v[...]).astype(BF16).astype(F32)
            kg = kg + jnp.sum(up * k * scale, axis=0, keepdims=True)
            u = up * kgain[...]
            mean = jnp.sum(u * k, axis=1, keepdims=True) * (1.0 / HD)
            gk = (scale * u - k * (scale * scale * scale) * mean).astype(BF16)
            gkbuf[ds(me * ROWS, ROWS, ROWS), head] = gk
            if n + s == 0:
                msum_v[...] = gk.astype(F32) * k
            else:
                msum_v[...] += gk.astype(F32) * k
    gbuf1[me, :, D:] = kg

    for dz, dc in ((0, 1), (1, 0), (3, 0), (2, 0)):
        q, pc = lax.rem(g + dz, 4), lax.rem(c + dc, 2)
        remote(mine(gkbuf), mine(gkbuf), k_ss, k_rs.at[me], z_dev(q, pc)).start()
    for k in range(1, NC):
        send_h(k)

    mean = jnp.sum(msum_v[...], axis=1, keepdims=True) * (1.0 / D)
    msum_v[...] = jnp.broadcast_to(mean, (ROWS, HD))

    def send_slots(q, order):
        quarter = ds(q * 1280, 1280, 1280)
        for dx, dy, dc in order:
            dev = plane(lax.rem(x + dx, 4), lax.rem(y + dy, 4), lax.rem(c + dc, 2))
            remote(
                slots_v.at[ds(dev[1] * PAIR, PAIR, PAIR), quarter],
                slots_out.at[ds(l * PAIR, PAIR, PAIR), quarter],
                s_ss, s_rs, dev,
            ).start()

    def quarter_of(q):
        for s in range(1280 // TW):
            cols = pl.ds(pl.multiple_of(q * 1280 + s * TW, TW), TW)
            grad_h = lax.dot_general(
                mine(gkbuf)[...], w_v[cols, :], (((1,), (1,)), ((), ())), preferred_element_type=F32
            )
            inv = jnp.concatenate([inv_v[...]] * (TW // HD), axis=1)
            mean = jnp.concatenate([msum_v[...]] * (TW // HD), axis=1)
            normed = x_v[:, cols].astype(F32) * inv
            gbuf1[me, :, cols] = jnp.sum(grad_h * normed, axis=0, keepdims=True)
            grad_in = (inv * (grad_h * gain[:, cols] - normed * mean)).astype(BF16)
            slots_v[:, cols] = jnp.dot(place_v[...], grad_in, preferred_element_type=F32).astype(BF16)

    @pl.loop(0, 2)
    def _(q):
        quarter_of(q)
        send_slots(q, ORDER)

    @pl.loop(2, 4)
    def _(q):
        quarter_of(q)

    own_rows = ds(l * PAIR, PAIR, PAIR)
    own = pltpu.make_async_copy(slots_v.at[own_rows], slots_out.at[own_rows], own_sem)
    own.start()
    groups = (ORDER[:9], ORDER[9:17], ORDER[17:25], ORDER[25:])
    held_back = [(q, order) for q in (2, 3) for order in groups]

    def send_more(count):
        for _ in range(count):
            if held_back:
                send_slots(*held_back.pop(0))

    def broadcast(buf, place, peers, ss, rs):
        copies = []
        for i, dev in enumerate(peers):
            copy = remote(buf.at[place], buf.at[place], ss.at[i], rs.at[place], dev)
            copy.start()
            copies.append(copy)
        return copies

    def arrived(ref, rs):
        remote(ref, ref, rs, rs, (g, l)).wait_recv()

    g_copies = broadcast(
        gbuf1, me, [z_dev(lax.rem(g + dz, 4), lax.rem(c + dc, 2)) for dz, dc in ZPEERS], g1_ss, g1_rs
    )
    partner = z_dev(g, 1 - c)

    def of(ref, src):
        return ref.at[ds(src * ROWS, ROWS, ROWS)]

    for dz in (1, 3, 2):
        same = lax.rem(g + dz, 4) * 2 + c
        arrived(of(gkbuf, same), k_rs.at[same])
        remote(of(gkbuf, same), of(gkbuf, same), rel_ss, k_rs.at[same], partner).start()
    for dz in (0, 1, 3, 2):
        cross = lax.rem(g + dz, 4) * 2 + 1 - c
        arrived(of(gkbuf, cross), k_rs.at[cross])

    def stage0(k):
        for dz, dc in ZPEERS:
            src = lax.rem(g + dz, 4) * 2 + lax.rem(c + dc, 2)
            arrived(of(hbuf.at[k], src), h_rs.at[k, src])
        part = lax.dot_general(
            hbuf[k], gkbuf[...], (((0,), (0,)), ((), ())), preferred_element_type=F32
        )
        acc[k % 2] = part
        for n in range(4):
            rs1s[k, n] = part[:, n * 256 : (n + 1) * 256].astype(BF16)
        for d in (1, 3, 2):
            na = lax.rem(a + d, 4)
            remote(rs1s.at[k, na], rs1r.at[k, a], r1_ss, r1_rs.at[k, a], a_dev(na)).start()

    def stage1(k):
        total = acc[k % 2, :, ds(a * 256, 256, 256)]
        for d in (1, 3, 2):
            na = lax.rem(a + d, 4)
            arrived(rs1r.at[k, na], r1_rs.at[k, na])
            total = total + rs1r[k, na].astype(F32)
        tot_v[k % 2] = total
        rs2s[k] = total.astype(BF16)
        for d in (1, 3, 2):
            nb = lax.rem(b + d, 4)
            remote(
                rs2s.at[k, ds(nb * 32, 32, 32)], rs2r.at[k, b], r2_ss, r2_rs.at[k, b], b_dev(nb)
            ).start()

    def block(k, na, nb=None, pc=c):
        row = pc * PIECE + k * FC
        rows = ds(row, FC, FC) if nb is None else ds(row + nb * 32, 32, 32)
        return wbuf.at[rows, ds(na * 256, 256, 256)]

    def stage2(k):
        total = tot_v[k % 2, ds(b * 32, 32, 32), :]
        for d in (1, 3, 2):
            nb = lax.rem(b + d, 4)
            arrived(rs2r.at[k, nb], r2_rs.at[k, nb])
            total = total + rs2r[k, nb].astype(F32)
        final = block(k, a, b)
        final[...] = total.astype(BF16)
        for d in (1, 3, 2):
            remote(final, final, ab_ss, ab_rs.at[k, b], b_dev(lax.rem(b + d, 4))).start()

    def stage3(k):
        for d in (1, 3, 2):
            nb = lax.rem(b + d, 4)
            arrived(block(k, a, nb), ab_rs.at[k, nb])
        whole = block(k, a)
        for d in (1, 3, 2):
            remote(whole, whole, aa_ss, aa_rs.at[k, a], a_dev(lax.rem(a + d, 4))).start()
        remote(whole, whole, ac_ss, ac_rs.at[k, a], partner).start()

    def stage4(k):
        for d in (1, 3, 2):
            na = lax.rem(a + d, 4)
            whole = block(k, na)
            arrived(whole, aa_rs.at[k, na])
            remote(whole, whole, ac_ss, ac_rs.at[k, na], partner).start()

    def stage5(k):
        for n in range(4):
            arrived(block(k, n, pc=1 - c), ac_rs.at[k, n])

    stages = (stage0, stage1, stage2, stage3, stage4, stage5)
    for t in range(NC + len(stages) - 1):
        for i, stage in enumerate(stages):
            if 0 <= t - i < NC:
                stage(t - i)
        send_more(2)
        if t == 0:
            for dz, dc in ZPEERS:
                src = lax.rem(g + dz, 4) * 2 + lax.rem(c + dc, 2)
                arrived(gbuf1.at[src], g1_rs.at[src])
            total = gbuf1[0]
            for i in range(1, 8):
                total = total + gbuf1[i]
            gbuf2[x] = total
            g_copies += broadcast(
                gbuf2, x, [plane(lax.rem(x + d, 4), y, c) for d in (1, 3, 2)], g2_ss, g2_rs
            )
        if t == 3:
            for d in (1, 3, 2):
                px = lax.rem(x + d, 4)
                arrived(gbuf2.at[px], g2_rs.at[px])
            gbuf3[y] = (gbuf2[0] + gbuf2[1]) + (gbuf2[2] + gbuf2[3])
            g_copies += broadcast(
                gbuf3, y, [plane(x, lax.rem(y + d, 4), c) for d in (1, 3, 2)], g3_ss, g3_rs
            )
    out = pltpu.make_async_copy(wbuf, w_out, in_sem.at[0])
    out.start()

    for d in (1, 3, 2):
        py = lax.rem(y + d, 4)
        arrived(gbuf3.at[py], g3_rs.at[py])
    total = (gbuf3[0] + gbuf3[1]) + (gbuf3[2] + gbuf3[3])
    g_out[...] = total[:, :D]
    kg_out[...] = total[:, D:]

    def sent(ref, ss):
        remote(ref, ref, ss, ss, (g, l)).wait_send()

    for copy in g_copies:
        copy.wait_send()
    sent(hbuf.at[:, ds(0, 7 * ROWS)], h_ss)
    sent(gkbuf.at[ds(0, 4 * ROWS)], k_ss)
    sent(gkbuf.at[ds(0, 3 * ROWS)], rel_ss)
    sent(rs1s.at[:, ds(0, 3)], r1_ss)
    sent(rs2s.at[:, ds(0, 96)], r2_ss)
    sent(rs2s.at[:, ds(0, 96)], ab_ss)
    sent(rs1s.at[:, ds(0, 3)], aa_ss)
    sent(rs1s, ac_ss)
    own.wait()
    everyone = remote(slots_v.at[ds(0, 31 * PAIR)], slots_out.at[ds(0, 31 * PAIR)], s_ss, s_rs, (g, l))
    everyone.wait_send()
    everyone.wait_recv()
    out.wait()


def body(hidden, cotangent, importance, block_len, version, destination, w_key, in_gain, key_gain):
    dma = pltpu.SemaphoreType.DMA
    vmem = pl.BlockSpec(memory_space=pltpu.VMEM)
    hbm = pl.BlockSpec(memory_space=pl.ANY)
    slots, w_rows, gain_grad, kgain_grad = pl.pallas_call(
        kernel,
        name="grad_step",
        out_shape=(
            jax.ShapeDtypeStruct((SR, D), BF16),
            jax.ShapeDtypeStruct((D // 4, KD), BF16),
            jax.ShapeDtypeStruct((1, D), F32),
            jax.ShapeDtypeStruct((1, HD), F32),
        ),
        in_specs=[hbm, hbm, vmem, vmem, vmem, vmem, hbm, vmem, vmem],
        out_specs=(hbm, hbm, vmem, vmem),
        scratch_shapes=[
            pltpu.VMEM((ROWS, D), BF16),
            pltpu.VMEM((D, KD), BF16),
            pltpu.VMEM((ROWS, KD), BF16),
            pltpu.VMEM((ROWS, HD), F32),
            pltpu.VMEM((ROWS, HD), F32),
            pltpu.VMEM((ROWS, D), BF16),
            pltpu.VMEM((ROWS, HD), F32),
            pltpu.VMEM((SR, ROWS), BF16),
            pltpu.VMEM((SR, D), BF16),
            pltpu.VMEM((NC, 8 * ROWS, FC), BF16),
            pltpu.VMEM((8 * ROWS, KD), BF16),
            pltpu.VMEM((2, FC, KD), F32),
            pltpu.VMEM((2, FC, 256), F32),
            pltpu.VMEM((NC, 4, FC, 256), BF16),
            pltpu.VMEM((NC, 4, FC, 256), BF16),
            pltpu.VMEM((NC, FC, 256), BF16),
            pltpu.VMEM((NC, 4, 32, 256), BF16),
            pltpu.VMEM((D // 4, KD), BF16),
            pltpu.VMEM((8, 1, D + HD), F32),
            pltpu.VMEM((4, 1, D + HD), F32),
            pltpu.VMEM((4, 1, D + HD), F32),
            dma((5,)), dma((4,)), dma(()),
            dma(()), dma((NC, 8)), dma(()), dma((8,)), dma(()), dma(()), dma(()),
            dma(()), dma((NC, 4)), dma(()), dma((NC, 4)),
            dma(()), dma((NC, 4)), dma(()), dma((NC, 4)), dma(()), dma((NC, 4)),
            dma((7,)), dma((8,)), dma((3,)), dma((4,)), dma((3,)), dma((4,)),
        ],
        compiler_params=pltpu.CompilerParams(
            collective_id=0, has_side_effects=True, vmem_limit_bytes=50 * 1024 * 1024
        ),
    )(
        hidden, cotangent, importance.reshape(1, ROWS), block_len.reshape(1, 32),
        version.reshape(1, 32), destination.reshape(1, 32), w_key, in_gain.reshape(1, D), key_gain.reshape(1, HD),
    )
    return slots, w_rows.astype(F32), gain_grad[0], kgain_grad[0]


def solution(mesh):
    return jax.shard_map(
        body,
        mesh=mesh,
        in_specs=(
            P(("gen", "learn"), None),
            P(("gen", "learn"), None),
            P(("gen", "learn")),
            P(("gen", "learn")),
            P(("gen", "learn")),
            P(("gen", "learn"), None),
            P(),
            P(),
            P(),
        ),
        out_specs=(P(("gen", "learn"), None), P("gen", None), P(), P()),
        check_vma=False,
    )
```

time: 126 us -> 130 us (1.032)
  the two profiles are of different devices: /device:TPU:5 before, /device:TPU:1 now
where the time goes in v2:
time: 130 us
  Pallas kernels  116 us (89%)
  local copies, waits for them, and re-layouts  9.59 us (7%)
  other arithmetic  3.32 us (3%)
    pallas_call x1, Pallas kernels, body(): pl.pallas_call(kernel, name='grad_step', out_shape=(jax.ShapeDtypeStruct(...  116 us
    unnamed x19, local copies, waits for them, and re-layouts  9.59 us
    convert_element_type x1, other arithmetic, body(): return (slots, w_rows.astype(F32), gain_grad[0], kgain_grad[0])  3.32 us

profile of v2, /device:TPU:1, one launch (start us, length us, event | category | flops | bytes accessed | tf_op | source)
XLA Modules:
  0.0 129.9 jit_solution(4596347490695342846)
XLA Ops:
  0.6 0.0 copy-start
  0.6 1.0 copy-done
  1.7 0.0 copy-start.1
  1.7 0.7 copy-done.1
  2.4 0.0 copy-start.2
  2.4 0.7 copy-done.2
  3.1 0.0 copy-start.3
  3.1 0.7 copy-done.3
  3.7 0.0 copy-start.4
  3.7 0.7 copy-done.4
  4.4 0.0 copy-start.5
  4.4 0.7 copy-done.5
  5.1 0.0 copy-start.6
  5.1 0.7 copy-done.6
  5.7 116.3 %grad_step.1 = (bf16[512,5120]{1,0:T(8,128)(2,1)}, bf16[1280,1024]{1,0:T(8,128)(2,1)S(1)}, f32[1,5120]{1,0:T(1,128)S(1)}, f32[1,128]{1,0:T(1,128)S(1)}) custom-call(bf16[256,5120]{1,0:T(8,128)(2,1)} %hid.1, bf16[256,1024]{1,0:T(8,128)(2,1)S(1)} %copy-done, f32[1,256]{1,0:T(1,128)S(1)} %bitcast.10, s32[1,32]{1,0:T(1,128)S(1)} %bitcast.11, ...), custom_call_target="tpu_custom_call" | custom-call | tf_op jit(solution)/shard_map/grad_step/pallas_call | solution.py:379
  122.0 0.0 copy-start.7
  122.0 3.3 %convert_element_type.3 = f32[1280,1024]{1,0:T(8,128)} convert(bf16[1280,1024]{1,0:T(8,128)(2,1)S(1)} %get-tuple-element.9) | non-fusion elementwise | flops 1310720 | bytes 7864320 | tf_op jit(solution)/shard_map/convert_element_type | solution.py:425
  125.3 1.1 copy-done.7
  126.4 2.4 %copy.16 = bf16[512,5120]{1,0:T(8,128)(2,1)} copy(bf16[512,5120]{1,0:T(8,128)(2,1)S(1)} %copy-done.7) | data formatting | bytes 10485760
  128.8 0.6 copy.17
  129.4 0.5 copy.18
Async XLA Ops:
  0.6 1.0 copy-start
  1.7 0.7 copy-start.1
  2.4 0.7 copy-start.2
  3.1 0.7 copy-start.3
  3.7 0.7 copy-start.4
  4.4 0.7 copy-start.5
  5.1 0.7 copy-start.6
  122.0 4.4 %copy-start.7 = (bf16[512,5120]{1,0:T(8,128)(2,1)S(1)}, bf16[512,5120]{1,0:T(8,128)(2,1)}, u32[]{:S(2)}) copy-start(bf16[512,5120]{1,0:T(8,128)(2,1)} %get-tuple-element.16) | copy-start | bytes 15728644

commit v3 on v2

--- a/solution.py
+++ b/solution.py
@@ -32,15 +32,18 @@
 ZPEERS = ((0, 1), (1, 0), (3, 0), (1, 1), (3, 1), (2, 0), (2, 1))
 
 
+SLOT_GROUPS = (3, 2, 1, 1, 2, 2, 2, 1, 1, 1, 0)
+
+
 def ds(start, size, mult=None):
     return pl.ds(start if mult is None else pl.multiple_of(start, mult), size)
 
 
 def kernel(
     hid, cot, imp, blen, ver, dest, w, gain, kgain,
-    slots_out, w_out, g_out, kg_out,
+    slots_out, wbuf, g_out,
     x_v, w_v, cot_v, inv_v, cw_v, h_v, msum_v, place_v, slots_v, hbuf, gkbuf, acc, tot_v,
-    rs1s, rs1r, rs2s, rs2r, wbuf, gbuf1, gbuf2, gbuf3,
+    rs1s, rs1r, rs2s, rs2r, gbuf1, gbuf2, gbuf3,
     in_sem, w_sem, own_sem, h_ss, h_rs, k_ss, k_rs, rel_ss, s_ss, s_rs,
     r1_ss, r1_rs, r2_ss, r2_rs, ab_ss, ab_rs, aa_ss, aa_rs, ac_ss, ac_rs,
     g1_ss, g1_rs, g2_ss, g2_rs, g3_ss, g3_rs,
@@ -101,19 +104,6 @@
     age = 3.0 - ver_col
     decay = jnp.where(age == 0.0, 1.0, jnp.where(age == 1.0, 0.5, jnp.where(age == 2.0, 0.25, 0.125)))
     cw_v[...] = jnp.broadcast_to(jnp.minimum(imp_col, 2.0) * (decay * inside), (ROWS, HD))
-
-    b32 = lax.broadcasted_iota(jnp.int32, (32, 32), 0)
-    e32 = lax.broadcasted_iota(jnp.int32, (32, 32), 1)
-    dest_col = jnp.sum(jnp.where(b32 == e32, dest[...].astype(F32), 0.0), axis=1, keepdims=True)
-    blk = lax.broadcasted_iota(jnp.int32, (32, ROWS), 0)
-    row_blk = lax.broadcasted_iota(jnp.int32, (32, ROWS), 1) >> 3
-    dest_row = jnp.sum(jnp.where(blk == row_blk, dest_col, 0.0), axis=0, keepdims=True)
-    rank_row = jnp.sum(jnp.where((blk < row_blk) & (dest_col == dest_row), 1.0, 0.0), axis=0, keepdims=True)
-    target = dest_row * 2.0 + rank_row
-    srow = lax.broadcasted_iota(jnp.int32, (SR, ROWS), 0)
-    scol = lax.broadcasted_iota(jnp.int32, (SR, ROWS), 1)
-    hit = ((srow >> 3).astype(F32) == target) & ((srow & 7) == (scol & 7))
-    place_v[...] = jnp.where(hit, 1.0, 0.0).astype(BF16)
 
     @pl.loop(0, 4)
     def _(i):
@@ -136,8 +126,6 @@
                 cols = slice(f * HD, (f + 1) * HD)
                 h_v[rows, cols] = (x_v[rows, cols].astype(F32) * invs[k] * gain[:, cols]).astype(BF16)
 
-    pl.semaphore_wait(barrier, 31 + 6)
-
     def mine(ref):
         return ref.at[ds(me * ROWS, ROWS, ROWS)]
 
@@ -147,9 +135,19 @@
             piece = h_v.at[:, ds((q * 2 + pc) * PIECE + k * FC, FC, FC)]
             remote(piece, mine(hbuf.at[k]), h_ss, h_rs.at[k, me], z_dev(q, pc)).start()
 
-    send_h(0)
-    for k in range(NC):
-        hbuf[k, ds(me * ROWS, ROWS, ROWS), :] = h_v[:, ds(me * PIECE + k * FC, FC, FC)]
+    def place_rows():
+        b32 = lax.broadcasted_iota(jnp.int32, (32, 32), 0)
+        e32 = lax.broadcasted_iota(jnp.int32, (32, 32), 1)
+        dest_col = jnp.sum(jnp.where(b32 == e32, dest[...].astype(F32), 0.0), axis=1, keepdims=True)
+        blk = lax.broadcasted_iota(jnp.int32, (32, ROWS), 0)
+        row_blk = lax.broadcasted_iota(jnp.int32, (32, ROWS), 1) >> 3
+        dest_row = jnp.sum(jnp.where(blk == row_blk, dest_col, 0.0), axis=0, keepdims=True)
+        rank_row = jnp.sum(jnp.where((blk < row_blk) & (dest_col == dest_row), 1.0, 0.0), axis=0, keepdims=True)
+        target = dest_row * 2.0 + rank_row
+        srow = lax.broadcasted_iota(jnp.int32, (SR, ROWS), 0)
+        scol = lax.broadcasted_iota(jnp.int32, (SR, ROWS), 1)
+        hit = ((srow >> 3).astype(F32) == target) & ((srow & 7) == (scol & 7))
+        place_v[...] = jnp.where(hit, 1.0, 0.0).astype(BF16)
 
     pltpu.make_async_copy(cot, cot_v, in_sem.at[4]).wait()
     for n in range(4):
@@ -172,13 +170,18 @@
                 msum_v[...] = gk.astype(F32) * k
             else:
                 msum_v[...] += gk.astype(F32) * k
+        if n == 0:
+            pl.semaphore_wait(barrier, 31 + 6)
+            send_h(0)
+            place_rows()
     gbuf1[me, :, D:] = kg
 
-    for dz, dc in ((0, 1), (1, 0), (3, 0), (2, 0)):
+    for dz, dc in ((1, 0), (3, 0), (0, 1)):
         q, pc = lax.rem(g + dz, 4), lax.rem(c + dc, 2)
         remote(mine(gkbuf), mine(gkbuf), k_ss, k_rs.at[me], z_dev(q, pc)).start()
-    for k in range(1, NC):
-        send_h(k)
+    send_h(1)
+    for k in range(NC):
+        hbuf[k, ds(me * ROWS, ROWS, ROWS), :] = h_v[:, ds(me * PIECE + k * FC, FC, FC)]
 
     mean = jnp.sum(msum_v[...], axis=1, keepdims=True) * (1.0 / D)
     msum_v[...] = jnp.broadcast_to(mean, (ROWS, HD))
@@ -218,7 +221,7 @@
     own_rows = ds(l * PAIR, PAIR, PAIR)
     own = pltpu.make_async_copy(slots_v.at[own_rows], slots_out.at[own_rows], own_sem)
     own.start()
-    groups = (ORDER[:9], ORDER[9:17], ORDER[17:25], ORDER[25:])
+    groups = [ORDER[i : i + 4] for i in range(0, 31, 4)]
     held_back = [(q, order) for q in (2, 3) for order in groups]
 
     def send_more(count):
@@ -245,10 +248,22 @@
     def of(ref, src):
         return ref.at[ds(src * ROWS, ROWS, ROWS)]
 
-    for dz in (1, 3, 2):
-        same = lax.rem(g + dz, 4) * 2 + c
-        arrived(of(gkbuf, same), k_rs.at[same])
-        remote(of(gkbuf, same), of(gkbuf, same), rel_ss, k_rs.at[same], partner).start()
+    def hand_on(src, rows, dev):
+        ref = gkbuf.at[rows]
+        remote(ref, ref, rel_ss, k_rs.at[src], dev).start()
+
+    for step in (1, 3):
+        src = lax.rem(g + step, 4) * 2 + c
+        arrived(of(gkbuf, src), k_rs.at[src])
+        half = ds(src * ROWS + (step // 2) * (ROWS // 2), ROWS // 2, ROWS // 2)
+        hand_on(src, half, z_dev(lax.rem(g + 4 - step, 4), c))
+    for k in range(2, NC):
+        send_h(k)
+    for step in (1, 3, 2):
+        src = lax.rem(g + step, 4) * 2 + c
+        if step == 2:
+            arrived(of(gkbuf, src), k_rs.at[src])
+        hand_on(src, ds(src * ROWS, ROWS, ROWS), partner)
     for dz in (0, 1, 3, 2):
         cross = lax.rem(g + dz, 4) * 2 + 1 - c
         arrived(of(gkbuf, cross), k_rs.at[cross])
@@ -260,7 +275,7 @@
         part = lax.dot_general(
             hbuf[k], gkbuf[...], (((0,), (0,)), ((), ())), preferred_element_type=F32
         )
-        acc[k % 2] = part
+        acc[k % 3] = part
         for n in range(4):
             rs1s[k, n] = part[:, n * 256 : (n + 1) * 256].astype(BF16)
         for d in (1, 3, 2):
@@ -268,7 +283,7 @@
             remote(rs1s.at[k, na], rs1r.at[k, a], r1_ss, r1_rs.at[k, a], a_dev(na)).start()
 
     def stage1(k):
-        total = acc[k % 2, :, ds(a * 256, 256, 256)]
+        total = acc[k % 3, :, ds(a * 256, 256, 256)]
         for d in (1, 3, 2):
             na = lax.rem(a + d, 4)
             arrived(rs1r.at[k, na], r1_rs.at[k, na])
@@ -318,12 +333,14 @@
             arrived(block(k, n, pc=1 - c), ac_rs.at[k, n])
 
     stages = (stage0, stage1, stage2, stage3, stage4, stage5)
-    for t in range(NC + len(stages) - 1):
-        for i, stage in enumerate(stages):
-            if 0 <= t - i < NC:
-                stage(t - i)
-        send_more(2)
-        if t == 0:
+    lags = (0, 2, 3, 4, 5, 6)
+    for t in range(NC + lags[-1]):
+        for stage, lag in zip(stages, lags):
+            if 0 <= t - lag < NC:
+                stage(t - lag)
+            if lag == 0:
+                send_more(SLOT_GROUPS[t])
+        if t == 5:
             for dz, dc in ZPEERS:
                 src = lax.rem(g + dz, 4) * 2 + lax.rem(c + dc, 2)
                 arrived(gbuf1.at[src], g1_rs.at[src])
@@ -334,7 +351,7 @@
             g_copies += broadcast(
                 gbuf2, x, [plane(lax.rem(x + d, 4), y, c) for d in (1, 3, 2)], g2_ss, g2_rs
             )
-        if t == 3:
+        if t == 7:
             for d in (1, 3, 2):
                 px = lax.rem(x + d, 4)
                 arrived(gbuf2.at[px], g2_rs.at[px])
@@ -342,15 +359,11 @@
             g_copies += broadcast(
                 gbuf3, y, [plane(x, lax.rem(y + d, 4), c) for d in (1, 3, 2)], g3_ss, g3_rs
             )
-    out = pltpu.make_async_copy(wbuf, w_out, in_sem.at[0])
-    out.start()
-
     for d in (1, 3, 2):
         py = lax.rem(y + d, 4)
         arrived(gbuf3.at[py], g3_rs.at[py])
     total = (gbuf3[0] + gbuf3[1]) + (gbuf3[2] + gbuf3[3])
-    g_out[...] = total[:, :D]
-    kg_out[...] = total[:, D:]
+    g_out[...] = total
 
     def sent(ref, ss):
         remote(ref, ref, ss, ss, (g, l)).wait_send()
@@ -358,8 +371,8 @@
     for copy in g_copies:
         copy.wait_send()
     sent(hbuf.at[:, ds(0, 7 * ROWS)], h_ss)
-    sent(gkbuf.at[ds(0, 4 * ROWS)], k_ss)
-    sent(gkbuf.at[ds(0, 3 * ROWS)], rel_ss)
+    sent(gkbuf.at[ds(0, 3 * ROWS)], k_ss)
+    sent(gkbuf.at[ds(0, 4 * ROWS)], rel_ss)
     sent(rs1s.at[:, ds(0, 3)], r1_ss)
     sent(rs2s.at[:, ds(0, 96)], r2_ss)
     sent(rs2s.at[:, ds(0, 96)], ab_ss)
@@ -369,24 +382,40 @@
     everyone = remote(slots_v.at[ds(0, 31 * PAIR)], slots_out.at[ds(0, 31 * PAIR)], s_ss, s_rs, (g, l))
     everyone.wait_send()
     everyone.wait_recv()
-    out.wait()
+
+
+def finish(slots, w_rows, gains, slots_out, w_out, gain_out, kgain_out, f_v, sem):
+    copies = [
+        pltpu.make_async_copy(gains.at[:, ds(0, D)], gain_out, sem.at[0]),
+        pltpu.make_async_copy(gains.at[:, ds(D, HD)], kgain_out, sem.at[1]),
+        pltpu.make_async_copy(slots, slots_out, sem.at[2]),
+    ]
+    for copy in copies:
+        copy.start()
+    for i in range(4):
+        rows = slice(i * 320, (i + 1) * 320)
+        f_v[rows, :] = w_rows[rows, :].astype(F32)
+        copy = pltpu.make_async_copy(f_v.at[ds(i * 320, 320)], w_out.at[ds(i * 320, 320)], sem.at[3 + i])
+        copy.start()
+        copies.append(copy)
+    for copy in copies:
+        copy.wait()
 
 
 def body(hidden, cotangent, importance, block_len, version, destination, w_key, in_gain, key_gain):
     dma = pltpu.SemaphoreType.DMA
     vmem = pl.BlockSpec(memory_space=pltpu.VMEM)
     hbm = pl.BlockSpec(memory_space=pl.ANY)
-    slots, w_rows, gain_grad, kgain_grad = pl.pallas_call(
+    slots, w_rows, gains = pl.pallas_call(
         kernel,
         name="grad_step",
         out_shape=(
-            jax.ShapeDtypeStruct((SR, D), BF16),
-            jax.ShapeDtypeStruct((D // 4, KD), BF16),
-            jax.ShapeDtypeStruct((1, D), F32),
-            jax.ShapeDtypeStruct((1, HD), F32),
+            pltpu.VMEM((SR, D), BF16),
+            pltpu.VMEM((D // 4, KD), BF16),
+            pltpu.VMEM((1, D + HD), F32),
         ),
         in_specs=[hbm, hbm, vmem, vmem, vmem, vmem, hbm, vmem, vmem],
-        out_specs=(hbm, hbm, vmem, vmem),
+        out_specs=(vmem, vmem, vmem),
         scratch_shapes=[
             pltpu.VMEM((ROWS, D), BF16),
             pltpu.VMEM((D, KD), BF16),
@@ -399,13 +428,12 @@
             pltpu.VMEM((SR, D), BF16),
             pltpu.VMEM((NC, 8 * ROWS, FC), BF16),
             pltpu.VMEM((8 * ROWS, KD), BF16),
-            pltpu.VMEM((2, FC, KD), F32),
+            pltpu.VMEM((3, FC, KD), F32),
             pltpu.VMEM((2, FC, 256), F32),
             pltpu.VMEM((NC, 4, FC, 256), BF16),
             pltpu.VMEM((NC, 4, FC, 256), BF16),
             pltpu.VMEM((NC, FC, 256), BF16),
             pltpu.VMEM((NC, 4, 32, 256), BF16),
-            pltpu.VMEM((D // 4, KD), BF16),
             pltpu.VMEM((8, 1, D + HD), F32),
             pltpu.VMEM((4, 1, D + HD), F32),
             pltpu.VMEM((4, 1, D + HD), F32),
@@ -422,7 +450,24 @@
         hidden, cotangent, importance.reshape(1, ROWS), block_len.reshape(1, 32),
         version.reshape(1, 32), destination.reshape(1, 32), w_key, in_gain.reshape(1, D), key_gain.reshape(1, HD),
     )
-    return slots, w_rows.astype(F32), gain_grad[0], kgain_grad[0]
+    slots, w_grad, gain_grad, kgain_grad = pl.pallas_call(
+        finish,
+        name="finish",
+        out_shape=(
+            jax.ShapeDtypeStruct((SR, D), BF16),
+            jax.ShapeDtypeStruct((D // 4, KD), F32),
+            jax.ShapeDtypeStruct((1, D), F32),
+            jax.ShapeDtypeStruct((1, HD), F32),
+        ),
+        in_specs=[vmem, vmem, vmem],
+        out_specs=(hbm, hbm, hbm, hbm),
+        scratch_shapes=[
+            pltpu.VMEM((D // 4, KD), F32),
+            dma((7,)),
+        ],
+        compiler_params=pltpu.CompilerParams(vmem_limit_bytes=16 * 1024 * 1024),
+    )(slots, w_rows, gains)
+    return slots, w_grad, gain_grad[0], kgain_grad[0]
 
 
 def solution(mesh):

time: 130 us -> 106 us (0.82)
  Pallas kernels: 116 us -> 105 us
  local copies, waits for them, and re-layouts: 9.59 us -> 0 us
  other arithmetic: 3.32 us -> 0 us
    pallas_call x1 -> x2, Pallas kernels: 116 us -> 105 us  [the longest x1 101 us: body(): pl.pallas_call(kernel, name='grad_step', out_shape=(pltpu.VMEM((SR, D), B...]
    unnamed x19 -> x0, local copies, waits for them, and re-layouts: 9.59 us -> none
    convert_element_type x1 -> x0, other arithmetic: 3.32 us -> none  [body(): return (slots, w_rows.astype(F32), gain_grad[0], kgain_grad[0])]
where the time goes in v3:
time: 106 us; the launch traced here: 105 us
  Pallas kernels  105 us (99%)
    pallas_call x1, Pallas kernels, body(): pl.pallas_call(kernel, name='grad_step', out_shape=(pltpu.VMEM((SR, D), B...  101 us
    pallas_call x1, Pallas kernels, body(): pl.pallas_call(finish, name='finish', out_shape=(jax.ShapeDtypeStruct((SR...  4.04 us

profile of v3, /device:TPU:1, one launch (start us, length us, event | category | flops | bytes accessed | tf_op | source)
XLA Modules:
  0.0 105.4 jit_solution(17795751524780745962)
XLA Ops:
  0.6 100.6 %grad_step.1 = (bf16[512,5120]{1,0:T(8,128)(2,1)S(1)}, bf16[1280,1024]{1,0:T(8,128)(2,1)S(1)}, f32[1,5248]{1,0:T(1,128)S(1)}) custom-call(bf16[256,5120]{1,0:T(8,128)(2,1)} %hid.1, bf16[256,1024]{1,0:T(8,128)(2,1)} %cot.1, f32[1,256]{1,0:T(1,128)} %bitcast.9, s32[1,32]{1,0:T(1,128)} %bitcast.10, s32[1,32]{1,0:T(1,128)} %bitcast.11, s32[1,32]{1,0:T(1,128)} %bitcast.12, ...), custom_call_target="tpu_custom_call" | custom-call | tf_op jit(solution)/shard_map/grad_step/pallas_call | solution.py:409
  101.2 4.0 %finish.1 = (bf16[512,5120]{1,0:T(8,128)(2,1)}, f32[1280,1024]{1,0:T(8,128)}, f32[1,5120]{1,0:T(1,128)}, f32[1,128]{1,0:T(1,128)}) custom-call(bf16[512,5120]{1,0:T(8,128)(2,1)S(1)} %get-tuple-element.11.slots, bf16[1280,1024]{1,0:T(8,128)(2,1)S(1)} %get-tuple-element.12.w_rows, f32[1,5248]{1,0:T(1,128)S(1)} %get-tuple-element.13.gains), custom_call_target="tpu_custom_call" | custom-call | tf_op jit(solution)/shard_map/finish/pallas_call | solution.py:453

commit v4 on v3

--- a/solution.py
+++ b/solution.py
@@ -28,11 +28,20 @@
     (1, 0), (3, 0), (0, 1), (0, 3), (1, 1), (3, 3), (1, 3), (3, 1),
     (2, 0), (0, 2), (2, 1), (1, 2), (2, 3), (3, 2), (2, 2),
 )
-ORDER = ((0, 0, 1),) + tuple((a, b, c) for (a, b) in OTHERS for c in range(2))
+EARLY = ((2, 2, 0), (2, 2, 1), (2, 0, 0), (0, 2, 0))
+ORDER = ((0, 0, 1),) + tuple(
+    (a, b, c) for (a, b) in OTHERS for c in range(2) if (a, b, c) not in EARLY
+)
 ZPEERS = ((0, 1), (1, 0), (3, 0), (1, 1), (3, 1), (2, 0), (2, 1))
 
 
-SLOT_GROUPS = (3, 2, 1, 1, 2, 2, 2, 1, 1, 1, 0)
+MORE, GAINS = -1, -2
+PLAN = (
+    (0, 0), (MORE, 3), (0, 1), (MORE, 2), (0, 2), (MORE, 1), (1, 0), (0, 3), (MORE, 1), (1, 1), (2, 0),
+    (0, 4), (MORE, 2), (1, 2), (1, 3), (MORE, 2), (1, 4), (GAINS, 0), (2, 1), (2, 2), (MORE, 2),
+    (2, 3), (2, 4), (MORE, 2), (3, 0), (3, 1), (3, 2), (3, 3), (3, 4), (GAINS, 1), (MORE, 1),
+    (4, 0), (4, 1), (4, 2), (4, 3), (4, 4), (5, 0), (5, 1), (5, 2), (5, 3), (5, 4),
+)
 
 
 def ds(start, size, mult=None):
@@ -40,10 +49,13 @@
 
 
 def kernel(
-    hid, cot, imp, blen, ver, dest, w, gain, kgain,
+    hid, cot, imp_h, blen_h, ver_h, dest_h, w, gain_h, kgain_h,
     slots_out, wbuf, g_out,
     x_v, w_v, cot_v, inv_v, cw_v, h_v, msum_v, place_v, slots_v, hbuf, gkbuf, acc, tot_v,
     rs1s, rs1r, rs2s, rs2r, gbuf1, gbuf2, gbuf3,
+    imp, blen, ver, dest, gain, kgain,
+    early_place, early_xs, early_ks, early_x, early_k, early_inv, early_sum, early_g,
+    ex_ss, ex_rs, ek_ss, ek_rs,
     in_sem, w_sem, own_sem, h_ss, h_rs, k_ss, k_rs, rel_ss, s_ss, s_rs,
     r1_ss, r1_rs, r2_ss, r2_rs, ab_ss, ab_rs, aa_ss, aa_rs, ac_ss, ac_rs,
     g1_ss, g1_rs, g2_ss, g2_rs, g3_ss, g3_rs,
@@ -72,13 +84,23 @@
     def remote(src, dst, ss, rs, dev):
         return pltpu.make_async_remote_copy(src, dst, ss, rs, device_id=dev, device_id_type=MESH)
 
+    small = [
+        pltpu.make_async_copy(src, dst, in_sem.at[5 + i])
+        for i, (src, dst) in enumerate(
+            ((gain_h, gain), (imp_h, imp), (blen_h, blen), (ver_h, ver), (dest_h, dest), (kgain_h, kgain))
+        )
+    ]
+    for copy in small:
+        copy.start()
     for i in range(4):
         rows = ds(i * 64, 64)
         pltpu.make_async_copy(hid.at[rows], x_v.at[rows], in_sem.at[i]).start()
-    for n in range(4):
+
+    def load_w(n):
         cols = ds(n * 256, 256)
-        pltpu.make_async_copy(w.at[:, cols], w_v.at[:, cols], w_sem.at[n]).start()
-    pltpu.make_async_copy(cot, cot_v, in_sem.at[4]).start()
+        return pltpu.make_async_copy(w.at[:, cols], w_v.at[:, cols], w_sem.at[n])
+
+    load_w(0).start()
 
     barrier = pltpu.get_barrier_semaphore()
 
@@ -90,6 +112,9 @@
         pl.semaphore_signal(
             barrier, inc=1, device_id=z_dev(lax.rem(g + dz, 4), lax.rem(c + dc, 2)), device_id_type=MESH
         )
+
+    for copy in small:
+        copy.wait()
 
     r256 = lax.broadcasted_iota(jnp.int32, (ROWS, ROWS), 0)
     j256 = lax.broadcasted_iota(jnp.int32, (ROWS, ROWS), 1)
@@ -104,6 +129,19 @@
     age = 3.0 - ver_col
     decay = jnp.where(age == 0.0, 1.0, jnp.where(age == 1.0, 0.5, jnp.where(age == 2.0, 0.25, 0.125)))
     cw_v[...] = jnp.broadcast_to(jnp.minimum(imp_col, 2.0) * (decay * inside), (ROWS, HD))
+
+    b32 = lax.broadcasted_iota(jnp.int32, (32, 32), 0)
+    e32 = lax.broadcasted_iota(jnp.int32, (32, 32), 1)
+    dest_col = jnp.sum(jnp.where(b32 == e32, dest[...].astype(F32), 0.0), axis=1, keepdims=True)
+    blk = lax.broadcasted_iota(jnp.int32, (32, ROWS), 0)
+    row_blk = lax.broadcasted_iota(jnp.int32, (32, ROWS), 1) >> 3
+    dest_row = jnp.sum(jnp.where(blk == row_blk, dest_col, 0.0), axis=0, keepdims=True)
+    rank_row = jnp.sum(jnp.where((blk < row_blk) & (dest_col == dest_row), 1.0, 0.0), axis=0, keepdims=True)
+    target = dest_row * 2.0 + rank_row
+    srow = lax.broadcasted_iota(jnp.int32, (SR, ROWS), 0)
+    scol = lax.broadcasted_iota(jnp.int32, (SR, ROWS), 1)
+    hit = ((srow >> 3).astype(F32) == target) & ((srow & 7) == (scol & 7))
+    place_v[...] = jnp.where(hit, 1.0, 0.0).astype(BF16)
 
     @pl.loop(0, 4)
     def _(i):
@@ -126,6 +164,9 @@
                 cols = slice(f * HD, (f + 1) * HD)
                 h_v[rows, cols] = (x_v[rows, cols].astype(F32) * invs[k] * gain[:, cols]).astype(BF16)
 
+    load_w(1).start()
+    pltpu.make_async_copy(cot, cot_v, in_sem.at[4]).start()
+
     def mine(ref):
         return ref.at[ds(me * ROWS, ROWS, ROWS)]
 
@@ -135,26 +176,34 @@
             piece = h_v.at[:, ds((q * 2 + pc) * PIECE + k * FC, FC, FC)]
             remote(piece, mine(hbuf.at[k]), h_ss, h_rs.at[k, me], z_dev(q, pc)).start()
 
-    def place_rows():
-        b32 = lax.broadcasted_iota(jnp.int32, (32, 32), 0)
-        e32 = lax.broadcasted_iota(jnp.int32, (32, 32), 1)
-        dest_col = jnp.sum(jnp.where(b32 == e32, dest[...].astype(F32), 0.0), axis=1, keepdims=True)
-        blk = lax.broadcasted_iota(jnp.int32, (32, ROWS), 0)
-        row_blk = lax.broadcasted_iota(jnp.int32, (32, ROWS), 1) >> 3
-        dest_row = jnp.sum(jnp.where(blk == row_blk, dest_col, 0.0), axis=0, keepdims=True)
-        rank_row = jnp.sum(jnp.where((blk < row_blk) & (dest_col == dest_row), 1.0, 0.0), axis=0, keepdims=True)
-        target = dest_row * 2.0 + rank_row
-        srow = lax.broadcasted_iota(jnp.int32, (SR, ROWS), 0)
-        scol = lax.broadcasted_iota(jnp.int32, (SR, ROWS), 1)
-        hit = ((srow >> 3).astype(F32) == target) & ((srow & 7) == (scol & 7))
-        place_v[...] = jnp.where(hit, 1.0, 0.0).astype(BF16)
+    early = [
+        plane(lax.rem(x + dx, 4), lax.rem(y + dy, 4), lax.rem(c + dc, 2)) for dx, dy, dc in EARLY
+    ]
+
+    def of_early(e):
+        return ds(e * PAIR, PAIR)
+
+    def send_early(src, dst, ss, rs):
+        for e, dev in enumerate(early):
+            remote(src.at[of_early(e)], dst.at[of_early(e)], ss, rs.at[e], dev).start()
+
+    for e, dev in enumerate(early):
+        early_place[of_early(e), :] = place_v[ds(dev[1] * PAIR, PAIR, PAIR), :]
+    for f in range(0, D, TW):
+        early_xs[:, f : f + TW] = jnp.dot(
+            early_place[...], x_v[:, f : f + TW], preferred_element_type=F32
+        ).astype(BF16)
+
+    load_w(2).start()
+    load_w(3).start()
+    pl.semaphore_wait(barrier, 31 + 6)
+    send_early(early_xs, early_x, ex_ss, ex_rs)
+    send_h(0)
 
     pltpu.make_async_copy(cot, cot_v, in_sem.at[4]).wait()
-    for n in range(4):
-        cols = ds(n * 256, 256)
-        pltpu.make_async_copy(w.at[:, cols], w_v.at[:, cols], w_sem.at[n]).wait()
     kg = jnp.zeros((1, HD), F32)
     for n in range(4):
+        load_w(n).wait()
         keys = jnp.dot(h_v[...], w_v[:, n * 256 : (n + 1) * 256], preferred_element_type=F32)
         for s in range(2):
             k = keys[:, s * HD : (s + 1) * HD]
@@ -170,15 +219,13 @@
                 msum_v[...] = gk.astype(F32) * k
             else:
                 msum_v[...] += gk.astype(F32) * k
-        if n == 0:
-            pl.semaphore_wait(barrier, 31 + 6)
-            send_h(0)
-            place_rows()
     gbuf1[me, :, D:] = kg
 
     for dz, dc in ((1, 0), (3, 0), (0, 1)):
         q, pc = lax.rem(g + dz, 4), lax.rem(c + dc, 2)
         remote(mine(gkbuf), mine(gkbuf), k_ss, k_rs.at[me], z_dev(q, pc)).start()
+    early_ks[...] = jnp.dot(early_place[...], mine(gkbuf)[...], preferred_element_type=F32).astype(BF16)
+    send_early(early_ks, early_k, ek_ss, ek_rs)
     send_h(1)
     for k in range(NC):
         hbuf[k, ds(me * ROWS, ROWS, ROWS), :] = h_v[:, ds(me * PIECE + k * FC, FC, FC)]
@@ -221,7 +268,7 @@
     own_rows = ds(l * PAIR, PAIR, PAIR)
     own = pltpu.make_async_copy(slots_v.at[own_rows], slots_out.at[own_rows], own_sem)
     own.start()
-    groups = [ORDER[i : i + 4] for i in range(0, 31, 4)]
+    groups = [ORDER[i : i + 4] for i in range(0, len(ORDER), 4)]
     held_back = [(q, order) for q in (2, 3) for order in groups]
 
     def send_more(count):
@@ -259,7 +306,51 @@
         hand_on(src, half, z_dev(lax.rem(g + 4 - step, 4), c))
     for k in range(2, NC):
         send_h(k)
-    for step in (1, 3, 2):
+    for step in (1, 3):
+        src = lax.rem(g + step, 4) * 2 + c
+        hand_on(src, ds(src * ROWS, ROWS, ROWS), partner)
+
+    for e in range(len(EARLY)):
+        arrived(early_x.at[of_early(e)], ex_rs.at[e])
+        arrived(early_k.at[of_early(e)], ek_rs.at[e])
+    invs = []
+    for e in range(len(EARLY)):
+        total = jnp.zeros((PAIR, HD), F32)
+        for f in range(0, D, HD):
+            xf = early_x[of_early(e), f : f + HD].astype(F32)
+            total = total + xf * xf
+        invs.append(lax.rsqrt(jnp.sum(total, axis=1, keepdims=True) * (1.0 / D) + EPS))
+    early_inv[...] = jnp.broadcast_to(jnp.concatenate(invs, axis=0), (len(EARLY) * PAIR, HD))
+    early_sum[...] = jnp.zeros_like(early_sum)
+
+    @pl.loop(0, D // 1024)
+    def _(i):
+        inv = jnp.concatenate([early_inv[...]] * 2, axis=1)
+        for s in range(4):
+            cols = pl.ds(pl.multiple_of(i * 1024 + s * TW, TW), TW)
+            grad_h = lax.dot_general(
+                early_k[...], w_v[cols, :], (((1,), (1,)), ((), ())), preferred_element_type=F32
+            )
+            grad = grad_h * gain[:, cols]
+            early_g[:, cols] = grad
+            prod = grad * (early_x[:, cols].astype(F32) * inv)
+            early_sum[...] += prod[:, :HD] + prod[:, HD:]
+
+    mean = jnp.sum(early_sum[...], axis=1, keepdims=True) * (1.0 / D)
+    early_sum[...] = jnp.broadcast_to(mean, early_sum.shape)
+
+    @pl.loop(0, D // 1280)
+    def _(i):
+        for e, dev in enumerate(early):
+            for s in range(1280 // HD):
+                cols = pl.ds(pl.multiple_of(i * 1280 + s * HD, HD), HD)
+                rows = of_early(e)
+                inv = early_inv[rows, :]
+                normed = early_x[rows, cols].astype(F32) * inv
+                grad_in = inv * (early_g[rows, cols] - normed * early_sum[rows, :])
+                slots_out[ds(dev[1] * PAIR, PAIR, PAIR), cols] = grad_in.astype(BF16)
+
+    for step in (2,):
         src = lax.rem(g + step, 4) * 2 + c
         if step == 2:
             arrived(of(gkbuf, src), k_rs.at[src])
@@ -275,7 +366,7 @@
         part = lax.dot_general(
             hbuf[k], gkbuf[...], (((0,), (0,)), ((), ())), preferred_element_type=F32
         )
-        acc[k % 3] = part
+        acc[k % 4] = part
         for n in range(4):
             rs1s[k, n] = part[:, n * 256 : (n + 1) * 256].astype(BF16)
         for d in (1, 3, 2):
@@ -283,12 +374,12 @@
             remote(rs1s.at[k, na], rs1r.at[k, a], r1_ss, r1_rs.at[k, a], a_dev(na)).start()
 
     def stage1(k):
-        total = acc[k % 3, :, ds(a * 256, 256, 256)]
+        total = acc[k % 4, :, ds(a * 256, 256, 256)]
         for d in (1, 3, 2):
             na = lax.rem(a + d, 4)
             arrived(rs1r.at[k, na], r1_rs.at[k, na])
             total = total + rs1r[k, na].astype(F32)
-        tot_v[k % 2] = total
+        tot_v[k] = total
         rs2s[k] = total.astype(BF16)
         for d in (1, 3, 2):
             nb = lax.rem(b + d, 4)
@@ -302,7 +393,7 @@
         return wbuf.at[rows, ds(na * 256, 256, 256)]
 
     def stage2(k):
-        total = tot_v[k % 2, ds(b * 32, 32, 32), :]
+        total = tot_v[k, ds(b * 32, 32, 32), :]
         for d in (1, 3, 2):
             nb = lax.rem(b + d, 4)
             arrived(rs2r.at[k, nb], r2_rs.at[k, nb])
@@ -332,33 +423,32 @@
         for n in range(4):
             arrived(block(k, n, pc=1 - c), ac_rs.at[k, n])
 
+    def gains_over_x():
+        for dz, dc in ZPEERS:
+            src = lax.rem(g + dz, 4) * 2 + lax.rem(c + dc, 2)
+            arrived(gbuf1.at[src], g1_rs.at[src])
+        total = gbuf1[0]
+        for i in range(1, 8):
+            total = total + gbuf1[i]
+        gbuf2[x] = total
+        return broadcast(gbuf2, x, [plane(lax.rem(x + d, 4), y, c) for d in (1, 3, 2)], g2_ss, g2_rs)
+
+    def gains_over_y():
+        for d in (1, 3, 2):
+            px = lax.rem(x + d, 4)
+            arrived(gbuf2.at[px], g2_rs.at[px])
+        gbuf3[y] = (gbuf2[0] + gbuf2[1]) + (gbuf2[2] + gbuf2[3])
+        return broadcast(gbuf3, y, [plane(x, lax.rem(y + d, 4), c) for d in (1, 3, 2)], g3_ss, g3_rs)
+
     stages = (stage0, stage1, stage2, stage3, stage4, stage5)
-    lags = (0, 2, 3, 4, 5, 6)
-    for t in range(NC + lags[-1]):
-        for stage, lag in zip(stages, lags):
-            if 0 <= t - lag < NC:
-                stage(t - lag)
-            if lag == 0:
-                send_more(SLOT_GROUPS[t])
-        if t == 5:
-            for dz, dc in ZPEERS:
-                src = lax.rem(g + dz, 4) * 2 + lax.rem(c + dc, 2)
-                arrived(gbuf1.at[src], g1_rs.at[src])
-            total = gbuf1[0]
-            for i in range(1, 8):
-                total = total + gbuf1[i]
-            gbuf2[x] = total
-            g_copies += broadcast(
-                gbuf2, x, [plane(lax.rem(x + d, 4), y, c) for d in (1, 3, 2)], g2_ss, g2_rs
-            )
-        if t == 7:
-            for d in (1, 3, 2):
-                px = lax.rem(x + d, 4)
-                arrived(gbuf2.at[px], g2_rs.at[px])
-            gbuf3[y] = (gbuf2[0] + gbuf2[1]) + (gbuf2[2] + gbuf2[3])
-            g_copies += broadcast(
-                gbuf3, y, [plane(x, lax.rem(y + d, 4), c) for d in (1, 3, 2)], g3_ss, g3_rs
-            )
+    for what, n in PLAN:
+        if what == MORE:
+            send_more(n)
+        elif what == GAINS:
+            g_copies += (gains_over_x, gains_over_y)[n]()
+        else:
+            stages[what](n)
+
     for d in (1, 3, 2):
         py = lax.rem(y + d, 4)
         arrived(gbuf3.at[py], g3_rs.at[py])
@@ -379,7 +469,10 @@
     sent(rs1s.at[:, ds(0, 3)], aa_ss)
     sent(rs1s, ac_ss)
     own.wait()
-    everyone = remote(slots_v.at[ds(0, 31 * PAIR)], slots_out.at[ds(0, 31 * PAIR)], s_ss, s_rs, (g, l))
+    sent(early_xs, ex_ss)
+    sent(early_ks, ek_ss)
+    rest = ds(0, len(ORDER) * PAIR)
+    everyone = remote(slots_v.at[rest], slots_out.at[rest], s_ss, s_rs, (g, l))
     everyone.wait_send()
     everyone.wait_recv()
 
@@ -414,7 +507,7 @@
             pltpu.VMEM((D // 4, KD), BF16),
             pltpu.VMEM((1, D + HD), F32),
         ),
-        in_specs=[hbm, hbm, vmem, vmem, vmem, vmem, hbm, vmem, vmem],
+        in_specs=[hbm] * 9,
         out_specs=(vmem, vmem, vmem),
         scratch_shapes=[
             pltpu.VMEM((ROWS, D), BF16),
@@ -428,8 +521,8 @@
             pltpu.VMEM((SR, D), BF16),
             pltpu.VMEM((NC, 8 * ROWS, FC), BF16),
             pltpu.VMEM((8 * ROWS, KD), BF16),
-            pltpu.VMEM((3, FC, KD), F32),
-            pltpu.VMEM((2, FC, 256), F32),
+            pltpu.VMEM((4, FC, KD), F32),
+            pltpu.VMEM((NC, FC, 256), F32),
             pltpu.VMEM((NC, 4, FC, 256), BF16),
             pltpu.VMEM((NC, 4, FC, 256), BF16),
             pltpu.VMEM((NC, FC, 256), BF16),
@@ -437,7 +530,22 @@
             pltpu.VMEM((8, 1, D + HD), F32),
             pltpu.VMEM((4, 1, D + HD), F32),
             pltpu.VMEM((4, 1, D + HD), F32),
-            dma((5,)), dma((4,)), dma(()),
+            pltpu.VMEM((1, ROWS), F32),
+            pltpu.VMEM((1, 32), jnp.int32),
+            pltpu.VMEM((1, 32), jnp.int32),
+            pltpu.VMEM((1, 32), jnp.int32),
+            pltpu.VMEM((1, D), F32),
+            pltpu.VMEM((1, HD), F32),
+            pltpu.VMEM((len(EARLY) * PAIR, ROWS), BF16),
+            pltpu.VMEM((len(EARLY) * PAIR, D), BF16),
+            pltpu.VMEM((len(EARLY) * PAIR, KD), BF16),
+            pltpu.VMEM((len(EARLY) * PAIR, D), BF16),
+            pltpu.VMEM((len(EARLY) * PAIR, KD), BF16),
+            pltpu.VMEM((len(EARLY) * PAIR, HD), F32),
+            pltpu.VMEM((len(EARLY) * PAIR, HD), F32),
+            pltpu.VMEM((len(EARLY) * PAIR, D), F32),
+            dma(()), dma((len(EARLY),)), dma(()), dma((len(EARLY),)),
+            dma((11,)), dma((4,)), dma(()),
             dma(()), dma((NC, 8)), dma(()), dma((8,)), dma(()), dma(()), dma(()),
             dma(()), dma((NC, 4)), dma(()), dma((NC, 4)),
             dma(()), dma((NC, 4)), dma(()), dma((NC, 4)), dma(()), dma((NC, 4)),

time: 106 us -> 97.7 us (0.922)
  Pallas kernels: 105 us -> 96.8 us
    pallas_call x1, Pallas kernels: 101 us -> 92.7 us  [body(): pl.pallas_call(kernel, name='grad_step', out_shape=(pltpu.VMEM((SR, D), B...]
where the time goes in v4:
time: 97.7 us; the launch traced here: 97.6 us
  Pallas kernels  96.8 us (99%)
    pallas_call x1, Pallas kernels, body(): pl.pallas_call(kernel, name='grad_step', out_shape=(pltpu.VMEM((SR, D), B...  92.7 us
    pallas_call x1, Pallas kernels, body(): pl.pallas_call(finish, name='finish', out_shape=(jax.ShapeDtypeStruct((SR...  4.04 us

profile of v4, /device:TPU:1, one launch (start us, length us, event | category | flops | bytes accessed | tf_op | source)
XLA Modules:
  0.0 97.6 jit_solution(16259964813522186562)
XLA Ops:
  0.6 92.7 %grad_step.1 = (bf16[512,5120]{1,0:T(8,128)(2,1)S(1)}, bf16[1280,1024]{1,0:T(8,128)(2,1)S(1)}, f32[1,5248]{1,0:T(1,128)S(1)}) custom-call(bf16[256,5120]{1,0:T(8,128)(2,1)} %hid.1, bf16[256,1024]{1,0:T(8,128)(2,1)} %cot.1, f32[1,256]{1,0:T(1,128)} %bitcast.9, s32[1,32]{1,0:T(1,128)} %bitcast.10, s32[1,32]{1,0:T(1,128)} %bitcast.11, s32[1,32]{1,0:T(1,128)} %bitcast.12, ...), custom_call_target="tpu_custom_call" | custom-call | tf_op jit(solution)/shard_map/grad_step/pallas_call | solution.py:502
  93.4 4.0 %finish.1 = (bf16[512,5120]{1,0:T(8,128)(2,1)}, f32[1280,1024]{1,0:T(8,128)}, f32[1,5120]{1,0:T(1,128)}, f32[1,128]{1,0:T(1,128)}) custom-call(bf16[512,5120]{1,0:T(8,128)(2,1)S(1)} %get-tuple-element.11.slots, bf16[1280,1024]{1,0:T(8,128)(2,1)S(1)} %get-tuple-element.12.w_rows, f32[1,5248]{1,0:T(1,128)S(1)} %get-tuple-element.13.gains), custom_call_target="tpu_custom_call" | custom-call | tf_op jit(solution)/shard_map/finish/pallas_call | solution.py:561

commit v5 on v4

--- a/solution.py
+++ b/solution.py
@@ -30,17 +30,18 @@
 )
 EARLY = ((2, 2, 0), (2, 2, 1), (2, 0, 0), (0, 2, 0))
 ORDER = ((0, 0, 1),) + tuple(
-    (a, b, c) for (a, b) in OTHERS for c in range(2) if (a, b, c) not in EARLY
+    (a, b, c) for c in range(2) for (a, b) in OTHERS if (a, b, c) not in EARLY
 )
 ZPEERS = ((0, 1), (1, 0), (3, 0), (1, 1), (3, 1), (2, 0), (2, 1))
 
 
 MORE, GAINS = -1, -2
 PLAN = (
-    (0, 0), (MORE, 3), (0, 1), (MORE, 2), (0, 2), (MORE, 1), (1, 0), (0, 3), (MORE, 1), (1, 1), (2, 0),
-    (0, 4), (MORE, 2), (1, 2), (1, 3), (MORE, 2), (1, 4), (GAINS, 0), (2, 1), (2, 2), (MORE, 2),
-    (2, 3), (2, 4), (MORE, 2), (3, 0), (3, 1), (3, 2), (3, 3), (3, 4), (GAINS, 1), (MORE, 1),
-    (4, 0), (4, 1), (4, 2), (4, 3), (4, 4), (5, 0), (5, 1), (5, 2), (5, 3), (5, 4),
+    (0, 0), (MORE, 3), (0, 1), (MORE, 2), (0, 2), (MORE, 1), (1, 0), (0, 3), (MORE, 1), (1, 1),
+    (2, 0), (0, 4), (MORE, 2), (1, 2), (2, 1), (3, 0), (1, 3), (MORE, 1), (1, 4), (GAINS, 0),
+    (2, 2), (3, 1), (MORE, 1), (2, 3), (4, 0), (2, 4), (MORE, 2), (3, 2), (4, 1), (3, 3), (3, 4),
+    (GAINS, 1), (MORE, 2), (4, 2), (4, 3), (4, 4), (MORE, 1), (5, 0), (5, 1), (5, 2), (5, 3),
+    (5, 4),
 )
 
 
@@ -481,8 +482,10 @@
     copies = [
         pltpu.make_async_copy(gains.at[:, ds(0, D)], gain_out, sem.at[0]),
         pltpu.make_async_copy(gains.at[:, ds(D, HD)], kgain_out, sem.at[1]),
-        pltpu.make_async_copy(slots, slots_out, sem.at[2]),
     ]
+    for i in range(4):
+        rows = ds(i * 128, 128)
+        copies.append(pltpu.make_async_copy(slots.at[rows], slots_out.at[rows], sem.at[7 + i]))
     for copy in copies:
         copy.start()
     for i in range(4):
@@ -571,7 +574,7 @@
         out_specs=(hbm, hbm, hbm, hbm),
         scratch_shapes=[
             pltpu.VMEM((D // 4, KD), F32),
-            dma((7,)),
+            dma((11,)),
         ],
         compiler_params=pltpu.CompilerParams(vmem_limit_bytes=16 * 1024 * 1024),
     )(slots, w_rows, gains)

time: 97.7 us -> 96.8 us (level)
  no operation moved by 1% of the time
where the time goes in v5:
time: 96.8 us; the launch traced here: 96.7 us
  Pallas kernels  95.9 us (99%)
    pallas_call x1, Pallas kernels, body(): pl.pallas_call(kernel, name='grad_step', out_shape=(pltpu.VMEM((SR, D), B...  91.8 us
    pallas_call x1, Pallas kernels, body(): pl.pallas_call(finish, name='finish', out_shape=(jax.ShapeDtypeStruct((SR...  4.07 us

profile of v5, /device:TPU:1, one launch (start us, length us, event | category | flops | bytes accessed | tf_op | source)
XLA Modules:
  0.0 96.7 jit_solution(17404737106558407388)
XLA Ops:
  0.6 91.8 %grad_step.1 = (bf16[512,5120]{1,0:T(8,128)(2,1)S(1)}, bf16[1280,1024]{1,0:T(8,128)(2,1)S(1)}, f32[1,5248]{1,0:T(1,128)S(1)}) custom-call(bf16[256,5120]{1,0:T(8,128)(2,1)} %hid.1, bf16[256,1024]{1,0:T(8,128)(2,1)} %cot.1, f32[1,256]{1,0:T(1,128)} %bitcast.9, s32[1,32]{1,0:T(1,128)} %bitcast.10, s32[1,32]{1,0:T(1,128)} %bitcast.11, s32[1,32]{1,0:T(1,128)} %bitcast.12, ...), custom_call_target="tpu_custom_call" | custom-call | tf_op jit(solution)/shard_map/grad_step/pallas_call | solution.py:505
  92.5 4.1 %finish.1 = (bf16[512,5120]{1,0:T(8,128)(2,1)}, f32[1280,1024]{1,0:T(8,128)}, f32[1,5120]{1,0:T(1,128)}, f32[1,128]{1,0:T(1,128)}) custom-call(bf16[512,5120]{1,0:T(8,128)(2,1)S(1)} %get-tuple-element.11.slots, bf16[1280,1024]{1,0:T(8,128)(2,1)S(1)} %get-tuple-element.12.w_rows, f32[1,5248]{1,0:T(1,128)S(1)} %get-tuple-element.13.gains), custom_call_target="tpu_custom_call" | custom-call | tf_op jit(solution)/shard_map/finish/pallas_call | solution.py:564
